TPU v7x, 32 devices: a whole 2x2x4 slice. The times are simulated.
32 devices in a mesh: tm: 4 (over y, x), dp: 8 (over z, core).
Axes of the slice: x: 2, y: 2, z: 4, core: 2. Of those that a mesh axis runs over, the one named last changes fastest.
Arguments:
- features: bfloat16 [8, 16, 2, 8, 256], P('dp', 'tm'), may hold values from -6 to 6
- upstream: bfloat16 [8, 16, 4, 16, 128], P('dp', 'tm'), may hold values from -6 to 6
- weight_one: bfloat16 [3, 3, 3, 256, 128], replicated, may hold values from -0.078125 to 0.078125
- weight_two: bfloat16 [3, 3, 3, 128, 128], replicated, may hold values from -0.109375 to 0.109375
Outputs:
- feature_grad: bfloat16 [8, 16, 2, 8, 256], P('dp', 'tm')
- grad_one: float32 [3, 3, 3, 256, 128], P(None, None, None, 'dp')
- grad_two: float32 [3, 3, 3, 128, 128], P(None, None, None, 'dp')
All inputs are finite; a program needn't handle non-finite values.
Results may differ from a plain program's by a relative error of at most 0.0049.
Values may be sent and summed in bfloat16 or wider, within the bound.
No kernel may reach another device: no remote copies, remote signals or barrier semaphores. Data moves between devices by JAX's collectives and lax.ppermute only.
A program may use at most 64 MiB of HBM per device.

v0:
```python
import math

import jax
import jax.numpy as jnp
from jax import lax
from jax.sharding import PartitionSpec as P


def passed_along(value, axis, by):
    size = lax.axis_size(axis)
    pairs = [(i, i + by) for i in range(size) if 0 <= i + by < size]
    return lax.ppermute(value, axis, pairs)


def upsample(values):
    return jnp.repeat(jnp.repeat(values, 2, axis=2), 2, axis=3)


def forward_conv(padded, kernel):
    return lax.conv_general_dilated(
        padded,
        kernel,
        (1, 1, 1),
        "VALID",
        dimension_numbers=("NDHWC", "DHWIO", "NDHWC"),
        preferred_element_type=jnp.float32,
    )


def kernel_grad(padded, cotangent):
    return lax.conv_general_dilated(
        padded,
        cotangent,
        (1, 1, 1),
        "VALID",
        dimension_numbers=("CDHWN", "IDHWO", "DHWNC"),
        preferred_element_type=jnp.float32,
    )


def data_grad(cotangent, kernel):
    return lax.conv_general_dilated(
        cotangent,
        kernel[::-1, ::-1, ::-1],
        (1, 1, 1),
        [(2, 2), (2, 2), (2, 2)],
        dimension_numbers=("NDHWC", "DHWOI", "NDHWC"),
        preferred_element_type=jnp.float32,
    )


def pad_space(values):
    return jnp.pad(values, ((0, 0), (0, 0), (1, 1), (1, 1), (0, 0)))


def pad_front(values, frames_dev):
    return jnp.pad(values, ((0, 0), (frames_dev - 2, 0), (0, 0), (0, 0), (0, 0)))


def silu_slope(pre):
    sigma = jax.nn.sigmoid(pre)
    return sigma * (1.0 + pre * (1.0 - sigma))


def pool_pairs(values):
    shape = values.shape
    return values.reshape(shape[0], shape[1], shape[2] // 2, 2, shape[3] // 2, 2, shape[4]).sum(
        axis=(3, 5)
    )


def on_device(features, upstream, weight_one, weight_two):
    frames_dev = features.shape[1]
    earlier = passed_along(features, "tm", 1)
    padded_all = pad_space(upsample(jnp.concatenate([earlier, features], axis=1)))
    pre_all = forward_conv(padded_all, weight_one)
    padded = padded_all[:, 2:]
    pre = pre_all[:, 2:]
    hidden_all = jax.nn.silu(pre_all).astype(jnp.bfloat16)
    grad_second = kernel_grad(pad_space(hidden_all), upstream)
    back_all = data_grad(upstream, weight_two)[:, :, 1:-1, 1:-1]
    later_back = passed_along(back_all[:, :2], "tm", -1)
    back = back_all[:, 2:] + pad_front(later_back, frames_dev)
    dpre = (back * silu_slope(pre)).astype(jnp.bfloat16)
    grad_first = kernel_grad(padded, dpre)
    pooled = pool_pairs(data_grad(dpre, weight_one)[:, :, 1:-1, 1:-1])
    later_pooled = passed_along(pooled[:, :2], "tm", -1)
    feature_grad = (pooled[:, 2:] + pad_front(later_pooled, frames_dev)).astype(jnp.bfloat16)
    totals = lax.psum((grad_first, grad_second), "tm")
    shares = (
        lax.psum_scatter(totals[0], "dp", scatter_dimension=3, tiled=True),
        lax.psum_scatter(totals[1], "dp", scatter_dimension=3, tiled=True),
    )
    count = (
        features.shape[0]
        * lax.axis_size("dp")
        * frames_dev
        * lax.axis_size("tm")
        * upstream.shape[2]
        * upstream.shape[3]
    )
    factor = 1.0 / math.sqrt(count)
    return (feature_grad, shares[0] * factor, shares[1] * factor)


def solution(mesh):
    in_specs = (P("dp", "tm", None, None, None), P("dp", "tm", None, None, None), P(), P())
    out_specs = (
        P("dp", "tm", None, None, None),
        P(None, None, None, "dp", None),
        P(None, None, None, "dp", None),
    )
    return jax.shard_map(
        on_device, mesh=mesh, in_specs=in_specs, out_specs=out_specs, check_vma=False
    )
```

profile of v0, /device:TPU:0, one launch (start us, length us, event | category | flops | bytes accessed | tf_op | source)
XLA Modules:
  0.0 162.8 jit_solution(198316848365468551)
XLA Ops:
  7.2 0.0 copy-start
  7.2 0.0 reduce-scatter.5.cloned.1.call-start
  7.2 5.0 %collective-permute-start.1 = (bf16[1,4,2,8,256]{4,3,2,1,0:T(8,128)(2,1)}, bf16[1,4,2,8,256]{4,3,2,1,0:T(8,128)(2,1)S(1)}, u32[]{:S(2)}, u32[]{:S(2)}) collective-permute-start(bf16[1,4,2,8,256]{4,3,2,1,0:T(8,128)(2,1)} %param.4), channel_id=1, source_target_pairs={{0,8},{8,16},{16,24},{1,9},{9,17},{17,25},{2,10},{10,18},{18,26},{... | collective-permute-start | bytes 98312 | tf_op jit(solution)/shard_map/ppermute | solution.py:12
  12.2 0.9 copy.47
  13.1 0.1 fusion.51
  13.2 0.0 copy-start.1
  13.2 2.4 %convolution_select_fusion.2 = f32[6,4,8,3,128]{4,2,3,1,0:T(8,128)S(1)} fusion(bf16[3,3,3,128,128]{4,3,2,1,0:T(8,128)(2,1)} %param.7, bf16[4,4,1,7,2,128]{5,3,4,1,0,2:T(8,128)(2,1)S(1)} %slice.43, bf16[4,4,1,8,3,128]{5,3,4,1,0,2:T(8,128)(2,1)S(1)} %copy.29, pred[8,3]{0,1:T(4,128)(4,1)} %constant.35), kind=kOutput, calls=%fused_computation.5 | convolution fusion | flops 283680768 | bytes 1335320 | tf_op jit(solution)/shard_map/slice | solution.py:81
  15.7 0.0 copy-start.2
  15.7 1.3 collective-permute-start
  17.0 0.1 copy.30
  17.1 0.0 collective-permute-done.1
  17.1 0.0 copy-done.1
  17.2 0.1 copy.34
  17.3 0.1 slice.48
  17.4 0.0 copy-done
  17.4 0.0 copy-done.2
  17.4 2.2 %fusion.31 = (bf16[6,4,8,3,128]{4,2,3,1,0:T(8,128)(2,1)S(1)}, f32[6,4,8,3,128]{4,2,3,1,0:T(8,128)S(1)}) fusion(pred[8,3]{0,1:T(4,128)(4,1)S(1)} %copy-done.2, bf16[3,3,3,256,128]{4,3,2,1,0:T(8,128)(2,1)S(1)} %copy-done, bf16[8,4,1,7,2,256]{5,3,4,1,0,2:T(8,128)(2,1)S(1)} %slice.48, bf16[8,4,1,8,3,256]{5,3,4,1,0,2:T(8,128)(2,1)S(1)} %copy.34), kind=kOutput, calls=%fused_computation.40 | convolution fusion | flops 851828736 | bytes 2834456 | tf_op jit(solution)/shard_map/conv_general_dilated | solution.py:20
  19.7 2.4 %convolution_bitcast_fusion = f32[3,3,3,128,128]{4,3,2,1,0:T(8,128)} fusion(bf16[4,4,8,3,128,1]{4,1,3,2,0,5:T(4,128)(2,1)S(1)} %bitcast.72, bf16[6,4,8,3,128,1]{4,2,3,1,0,5:T(8,128)(2,1)S(1)} %get-tuple-element.16, bf16[6,4,8,3,128,1]{4,2,3,1,0,5:T(8,128)(2,1)S(1)} %bitcast.62, bf16[6,4,8,3,128,1]{4,2,3,1,0,5:T(8,128)(2,1)S(1)} %get-tuple-element.17), kind=kOutput, calls=%fused_computation | convolution fusion | flops 283557888 | bytes 2310144 | tf_op jit(solution)/shard_map/conv_general_dilated | solution.py:31
  22.1 0.1 add_multiply_fusion
  22.2 0.1 copy.35
  22.3 0.0 reduce-scatter.5.cloned.1.call-update
  22.3 0.0 reduce-scatter.3.cloned.1.call-start
  22.3 0.0 collective-permute-done
  22.4 5.6 %fusion.7 = f32[3,3,3,256,128]{4,3,2,1,0:T(8,128)} fusion(bf16[1,8,4,16,256]{4,1,3,2,0:T(8,128)(2,1)S(1)} %bitcast.59, bf16[1,4,4,16,128]{4,2,3,1,0:T(4,128)(2,1)S(1)} %fusion.33), kind=kOutput, calls=%fused_computation.11 | convolution fusion | flops 361758720 | bytes 3866624 | tf_op jit(solution)/shard_map/conv_general_dilated | solution.py:31
  28.0 0.0 reduce-scatter.3.cloned.1.call-update
  28.1 0.0 all-reduce.5.cloned.1.call-start
  28.1 31.9 %reduce-scatter.5.cloned.1.call-done = f32[3,3,3,16,128]{4,3,2,1,0:T(8,128)} async-done(((f32[3,3,3,128,128]{4,3,2,1,0:T(8,128)}), f32[3,3,3,16,128]{4,3,2,1,0:T(8,128)}) %reduce-scatter.5.cloned.1.call-update) | async-done | bytes 221200 | tf_op jit(solution)/shard_map/reduce_scatter | solution.py:92
  60.1 44.0 %reduce-scatter.3.cloned.1.call-done = f32[3,3,3,32,128]{4,3,2,1,0:T(8,128)} async-done(((f32[3,3,3,256,128]{4,3,2,1,0:T(8,128)}), f32[3,3,3,32,128]{4,3,2,1,0:T(8,128)}) %reduce-scatter.3.cloned.1.call-update) | async-done | bytes 442384 | tf_op jit(solution)/shard_map/reduce_scatter | solution.py:91
  104.0 0.0 all-reduce.5.cloned.1.call-update
  104.2 1.3 convolution_select_fusion
  105.5 0.2 copy.40
  105.7 0.3 reshape.19
  106.1 0.3 reduce_sum.11
  106.4 1.3 collective-permute-start.2
  107.7 4.5 %collective-permute-done.2 = f32[1,2,2,8,256]{4,2,3,1,0:T(2,128)S(1)} collective-permute-done((f32[1,2,2,8,256]{4,2,3,1,0:T(2,128)S(1)}, f32[1,2,2,8,256]{4,2,3,1,0:T(2,128)S(1)}, u32[]{:S(2)}, u32[]{:S(2)}) %collective-permute-start.2) | collective-permute-done | bytes 32800 | tf_op jit(solution)/shard_map/ppermute | solution.py:12
  112.3 0.6 copy.46
  112.9 39.9 %all-reduce.5.cloned.1.call-done = (f32[3,3,3,32,128]{4,3,2,1,0:T(8,128)}, f32[3,3,3,16,128]{4,3,2,1,0:T(8,128)}) async-done(((f32[3,3,3,32,128]{4,3,2,1,0:T(8,128)}, f32[3,3,3,16,128]{4,3,2,1,0:T(8,128)}), (f32[3,3,3,32,128]{4,3,2,1,0:T(8,128)}, f32[3,3,3,16,128]{4,3,2,1,0:T(8,128)})) %all-reduce.5.cloned.1.call-update) | async-done | bytes 663568 | tf_op jit(solution)/shard_map/psum | solution.py:89
  152.8 1.8 %broadcast_multiply_fusion = f32[3,3,3,32,128]{4,3,2,1,0:T(8,128)} fusion(f32[3,3,3,32,128]{4,3,2,1,0:T(8,128)} %get-tuple-element.6), kind=kLoop, calls=%fused_computation.24 | loop fusion | flops 110592 | bytes 884736 | tf_op jit(solution)/shard_map/mul | solution.py:103
  154.6 1.6 %broadcast_multiply_fusion.1 = f32[3,3,3,16,128]{4,3,2,1,0:T(8,128)} fusion(f32[3,3,3,16,128]{4,3,2,1,0:T(8,128)} %get-tuple-element.7), kind=kLoop, calls=%fused_computation.47 | loop fusion | flops 55296 | bytes 442368 | tf_op jit(solution)/shard_map/mul | solution.py:103
  (23 shorter events, 0.5 us)
Async XLA Ops:
  7.2 10.2 %copy-start = (bf16[3,3,3,256,128]{4,3,2,1,0:T(8,128)(2,1)S(1)}, bf16[3,3,3,256,128]{4,3,2,1,0:T(8,128)(2,1)}, u32[]{:S(2)}) copy-start(bf16[3,3,3,256,128]{4,3,2,1,0:T(8,128)(2,1)} %param.6) | copy-start | bytes 5308420
  7.2 52.9 %reduce-scatter.5.cloned.1.call-start = ((), (), s32[]{:S(2)}) async-start(), calls=%async_computation.3 | async-start | bytes 1990656 | tf_op jit(solution)/shard_map/reduce_scatter | solution.py:92
  7.2 9.8 %collective-permute-start.1 = (bf16[1,4,2,8,256]{4,3,2,1,0:T(8,128)(2,1)}, bf16[1,4,2,8,256]{4,3,2,1,0:T(8,128)(2,1)S(1)}, u32[]{:S(2)}, u32[]{:S(2)}) collective-permute-start(bf16[1,4,2,8,256]{4,3,2,1,0:T(8,128)(2,1)} %param.4), channel_id=1, source_target_pairs={{0,8},{8,16},{16,24},{1,9},{9,17},{17,25},{2,10},{10,18},{18,26},{... | collective-permute-start | bytes 98312 | tf_op jit(solution)/shard_map/ppermute | solution.py:12
  13.2 3.9 %copy-start.1 = (bf16[1,4,2,8,256]{4,3,2,1,0:T(8,128)(2,1)S(1)}, bf16[1,4,2,8,256]{4,3,2,1,0:T(8,128)(2,1)}, u32[]{:S(2)}) copy-start(bf16[1,4,2,8,256]{4,3,2,1,0:T(8,128)(2,1)} %param.4) | copy-start | bytes 98308
  15.7 1.7 %copy-start.2 = (pred[8,3]{0,1:T(4,128)(4,1)S(1)}, pred[8,3]{0,1:T(4,128)(4,1)}, u32[]{:S(2)}) copy-start(pred[8,3]{0,1:T(4,128)(4,1)} %constant.35) | copy-start | bytes 76
  15.7 6.7 %collective-permute-start = (f32[1,2,4,16,128]{4,2,3,1,0:T(4,128)S(1)}, f32[1,2,4,16,128]{4,2,3,1,0:T(4,128)S(1)}, u32[]{:S(2)}, u32[]{:S(2)}) collective-permute-start(f32[1,2,4,16,128]{4,2,3,1,0:T(4,128)S(1)} %slice_bitcast_fusion.2), channel_id=1, source_target_pairs={{8,0},{16,8},{24,16},{9,1},{17,9},{25,17},{10,2},{18,10},{26,18},{... | collective-permute-start | bytes 196616 | tf_op jit(solution)/shard_map/ppermute | solution.py:12
  22.3 81.7 %reduce-scatter.3.cloned.1.call-start = ((), (), s32[]{:S(2)}) async-start(), calls=%async_computation.2 | async-start | bytes 3981312 | tf_op jit(solution)/shard_map/reduce_scatter | solution.py:91
  28.1 124.8 %all-reduce.5.cloned.1.call-start = ((), (), s32[]{:S(2)}) async-start(), calls=%async_computation.4 | async-start | bytes 1327104 | tf_op jit(solution)/shard_map/psum | solution.py:89
  106.4 5.8 %collective-permute-start.2 = (f32[1,2,2,8,256]{4,2,3,1,0:T(2,128)S(1)}, f32[1,2,2,8,256]{4,2,3,1,0:T(2,128)S(1)}, u32[]{:S(2)}, u32[]{:S(2)}) collective-permute-start(f32[1,2,2,8,256]{4,2,3,1,0:T(2,128)S(1)} %slice.54), channel_id=1, source_target_pairs={{8,0},{16,8},{24,16},{9,1},{17,9},{25,17},{10,2},{18,10},{26,18},{... | collective-permute-start | bytes 98312 | tf_op jit(solution)/shard_map/ppermute | solution.py:12
Sparse Core Ops, SparseCore 0:
  22.4 37.6 reduce-scatter.4
  62.4 41.6 reduce-scatter.2
  107.2 45.6 all-reduce.4
where the time goes:
time: 163 us
  waiting for transfers between devices  120 us (74%)
  between operations  14.1 us (9%)
  matrix products  13.9 us (9%)
  starting transfers between devices  7.71 us (5%)
  other arithmetic  4 us (2%)
  local copies, waits for them, and re-layouts  2.71 us (2%)
    reduce_scatter x1, waiting for transfers between devices, on_device(): lax.psum_scatter(totals[0], 'dp', scatter_dimension=3, tiled=True)  44 us
    psum x1, waiting for transfers between devices, on_device(): totals = lax.psum((grad_first, grad_second), 'tm')  39.9 us
    reduce_scatter x1, waiting for transfers between devices, on_device(): lax.psum_scatter(totals[1], 'dp', scatter_dimension=3, tiled=True)  31.9 us
    conv_general_dilated x2, matrix products, kernel_grad(): lax.conv_general_dilated(padded, cotangent, (1, 1, 1), 'VALID', dimension...  8.03 us
    ppermute x3, starting transfers between devices, passed_along(): return lax.ppermute(value, axis, pairs)  7.59 us
    ppermute x3, waiting for transfers between devices, passed_along(): return lax.ppermute(value, axis, pairs)  4.51 us
    mul x2, other arithmetic, on_device(): return (feature_grad, shares[0] * factor, shares[1] * factor)  3.46 us
  transfers between devices with their start and end apart: 6, of which 4 were waited for; matrix products, arithmetic and copies ran while one was open for 11% of the time, Pallas kernels for 0%

commit v1 on v0

v1 whole, which is shorter than its diff:
```python
import math

import jax
import jax.numpy as jnp
from jax import lax
from jax.experimental import pallas as pl
from jax.experimental.pallas import tpu as pltpu
from jax.sharding import PartitionSpec as P

F32, BF16 = jnp.float32, jnp.bfloat16


def swap(value, axis, hop, stride=1):
    size = lax.axis_size(axis)
    return lax.ppermute(value, axis, [(i, i ^ (hop * stride)) for i in range(size)])


def call(body, out_shape, name, scratch=(), flops=0):
    return pl.pallas_call(
        body,
        out_shape=out_shape,
        scratch_shapes=list(scratch),
        name=name,
        cost_estimate=pl.CostEstimate(flops=flops, transcendentals=0, bytes_accessed=0) if flops else None,
    )


def rows_of(value):
    return value.reshape(-1, value.shape[-1])


def move_down(value, fill_at):
    shape = value.shape
    flat = value.reshape(-1, shape[-2], shape[-1])
    by = 1 if fill_at == 0 else shape[-2] - 1
    turned = pltpu.roll(flat, by, 1)
    place = lax.broadcasted_iota(jnp.int32, turned.shape, 1)
    return jnp.where(place == fill_at, 0.0, turned).reshape(shape)


def pack_kernel(feats_ref, ups_ref, out_ref, wide):
    half = out_ref.shape[-1]
    low = feats_ref.shape[1]
    ins = feats_ref.shape[2] // half
    for part in range(ins):
        out_ref[:, part * low : (part + 1) * low, :] = feats_ref[:, :, part * half : (part + 1) * half]
    frames, ho, wo, _ = ups_ref.shape
    wide[...] = ups_ref[...].reshape(frames * ho, wo, half).astype(F32)
    even = wide[:, pl.ds(0, wo // 2, stride=2), :]
    odd = wide[:, pl.ds(1, wo // 2, stride=2), :]
    both = jnp.concatenate([even, odd], axis=1)
    out_ref[:, ins * low :, :] = both.reshape(frames, ho * wo, half).astype(BF16)


def main_kernel(dims, blocks, w1_ref, w2_ref, keep_ref, send_ref, dbox_ref, xs, uc, ht, ft, g1, g2):
    tm, dp, hi, wi, chunk = dims
    ho, wo = 2 * hi, 2 * wi
    low = hi * wi
    frames = blocks[0].shape[0]
    total = frames * tm
    cin, cout = w1_ref.shape[1], w1_ref.shape[2]
    parts = cin // cout
    me = lax.axis_index("tm")
    mine = lax.axis_index("dp")
    core, far = lax.rem(mine, 2), lax.div(mine, 2)

    xs[: 2 * low] = jnp.zeros((2 * low, cin), BF16)
    uc[:, total:] = jnp.zeros((3, 2) + uc.shape[2:], BF16)
    uc[:, :, 0] = jnp.zeros((3, total + 2) + uc.shape[3:], BF16)
    uc[:, :, ho + 1] = jnp.zeros((3, total + 2) + uc.shape[3:], BF16)
    for hop, block in enumerate(blocks):
        start = (me ^ hop) * frames
        feats = jnp.concatenate(
            [rows_of(block[:, part * low : (part + 1) * low, :]) for part in range(parts)], axis=1
        )
        xs[pl.ds(pl.multiple_of((start + 2) * low, low), frames * low), :] = feats
        ups = block[:, parts * low :, :].reshape(frames, ho, 2, wi, cout)
        wide = ups.astype(F32)
        even, odd = wide[:, :, 0], wide[:, :, 1]
        after = move_down(even, wi - 1)
        before = move_down(odd, 0)
        where = (pl.ds(start, frames), slice(1, ho + 1))
        uc[(0,) + where] = jnp.concatenate([odd, after], axis=2).astype(BF16)
        uc[(1,) + where] = block[:, parts * low :, :].reshape(frames, ho, wo, cout)
        uc[(2,) + where] = jnp.concatenate([before, even], axis=2).astype(BF16)

    by_row = []
    for b in range(3):
        sums = None
        for a in range(3):
            weight = jnp.concatenate([w1_ref[a * 9 + b * 3 + e] for e in range(3)], axis=1)
            term = jnp.dot(xs[a * low : (a + total) * low, :], weight, preferred_element_type=F32)
            sums = term if sums is None else sums + term
        by_row.append(sums.reshape(total, hi, wi, 3 * cout))
    zero = jnp.zeros((total, wi, 3 * cout), F32)
    pre_rows = []
    for row in range(hi):
        up = by_row[0][:, row - 1] if row else zero
        down = by_row[2][:, row + 1] if row + 1 < hi else zero
        pre_rows.append(up + by_row[1][:, row] + by_row[2][:, row])
        pre_rows.append(by_row[0][:, row] + by_row[1][:, row] + down)
    sums = jnp.stack(pre_rows, axis=1)
    first, middle, last = (sums[..., e * cout : (e + 1) * cout] for e in range(3))
    even = move_down(first, 0) + middle + last
    odd = first + middle + move_down(last, wi - 1)
    pre = jnp.concatenate([even, odd], axis=2)
    sigma = 1.0 / (1.0 + jnp.exp(-pre))
    hidden = pre * sigma
    slope = sigma * (1.0 + pre * (1.0 - sigma))
    ht[...] = rows_of(hidden).T.astype(BF16)
    ft[...] = xs[2 * low :, :].astype(F32).T.astype(BF16)

    back = None
    for a in range(3):
        for b in range(3):
            ups = jnp.concatenate(
                [rows_of(uc[e, 2 - a : 2 - a + total, 2 - b : 2 - b + ho]) for e in range(3)], axis=1
            )
            weight = jnp.concatenate([w2_ref[a * 9 + b * 3 + e] for e in range(3)], axis=1)
            term = lax.dot_general(ups, weight, (((1,), (1,)), ((), ())), preferred_element_type=F32)
            back = term if back is None else back + term
    dpre = (back.reshape(slope.shape) * slope).astype(BF16).astype(F32)
    even, odd = dpre[:, :, :wi], dpre[:, :, wi:]
    columns = (odd + move_down(even, wi - 1), even + odd, move_down(odd, 0) + even)
    for e in range(3):
        col = columns[e]
        for b in range(3):
            picked = []
            for row in range(hi):
                one, two = 2 * row + 1 - b, 2 * row + 2 - b
                value = None
                for at in (one, two):
                    if 0 <= at < ho:
                        value = col[:, at] if value is None else value + col[:, at]
                picked.append(value)
            box = jnp.concatenate(picked, axis=1)
            dbox_ref[b * 3 + e, :total] = box.astype(BF16)
    dbox_ref[:, total:] = jnp.zeros((9, 2, low, cout), BF16)

    far_size = dp // 2
    tall, short = cin // dp, cout // dp
    for j in range(chunk):
        tap = jnp.minimum(me * chunk + j, 26)
        a, rest = lax.div(tap, 9), lax.rem(tap, 9)
        b, e = lax.div(rest, 3), lax.rem(rest, 3)
        boxes = rows_of(dbox_ref[rest, pl.ds(2 - a, total)])
        g1[j] = jnp.dot(ft[...], boxes, preferred_element_type=F32)
        ups = rows_of(uc[e, pl.ds(2 - a, total), pl.ds(2 - b, ho)])
        g2[j] = jnp.dot(ht[...], ups, preferred_element_type=F32)
    for hop in range(far_size):
        for ref, side in ((keep_ref, core), (send_ref, 1 - core)):
            at = (far ^ hop) * 2 + side
            ref[hop, :, :tall] = g1[:, pl.ds(pl.multiple_of(at * tall, tall), tall)].astype(ref.dtype)
            ref[hop, :, tall:] = g2[:, pl.ds(pl.multiple_of(at * short, short), short)].astype(ref.dtype)


def input_grad_kernel(frames, dbox_ref, w1_ref, out_ref):
    start = lax.axis_index("tm") * frames
    total = None
    for a in range(3):
        for b in range(3):
            boxes = jnp.concatenate(
                [rows_of(dbox_ref[b * 3 + e, pl.ds(start + 2 - a, frames)]) for e in range(3)], axis=1
            )
            weight = jnp.concatenate([w1_ref[a * 9 + b * 3 + e] for e in range(3)], axis=1)
            term = lax.dot_general(boxes, weight, (((1,), (1,)), ((), ())), preferred_element_type=F32)
            total = term if total is None else total + term
    out_ref[...] = total.astype(BF16)


def pair_kernel(keep_ref, recv_ref, own_ref, *send_refs):
    own_ref[...] = keep_ref[0] + recv_ref[0].astype(F32)
    for hop, ref in enumerate(send_refs, 1):
        ref[...] = (keep_ref[hop] + recv_ref[hop].astype(F32)).astype(BF16)


def sum_kernel(factor, own_ref, *refs):
    *recv_refs, out_ref = refs
    total = own_ref[...]
    for ref in recv_refs:
        total += ref[...].astype(F32)
    out_ref[...] = (total * factor).astype(BF16)


def spread_kernel(tall, *refs):
    *in_refs, one_ref, two_ref = refs
    me = lax.axis_index("tm")
    chunk = in_refs[0].shape[0]
    taps = one_ref.shape[0]
    for hop, ref in enumerate(in_refs):
        for j in range(chunk):
            tap = (me ^ hop) * chunk + j

            @pl.when(tap < taps)
            def _():
                one_ref[tap] = ref[j, :tall].astype(F32)
                two_ref[tap] = ref[j, tall:].astype(F32)


def on_device(features, upstream, weight_one, weight_two):
    clips, frames, hi, wi, cin = features.shape
    ho, wo, cout = upstream.shape[2:]
    tm, dp = lax.axis_size("tm"), lax.axis_size("dp")
    taps = 27
    chunk = -(-taps // tm)
    total = frames * tm
    low, high = hi * wi, ho * wo
    far_size = dp // 2
    tall, short = cin // dp, cout // dp
    shape = jax.ShapeDtypeStruct
    w1 = weight_one.reshape(taps, cin, cout)
    w2 = weight_two.reshape(taps, cout, cout)

    packed = call(
        pack_kernel,
        shape((frames, low * (cin // cout) + high, cout), BF16),
        "pack",
        [pltpu.VMEM((frames * ho, wo, cout), F32)],
    )(features.reshape(frames, low, cin), upstream.reshape(frames, ho, wo, cout))
    blocks = [packed] + [swap(packed, "tm", hop) for hop in range(1, tm)]

    def main_body(*refs):
        main_kernel((tm, dp, hi, wi, chunk), refs[:tm], *refs[tm:])

    keep, send, dbox = call(
        main_body,
        (
            shape((far_size, chunk, tall + short, cout), F32),
            shape((far_size, chunk, tall + short, cout), BF16),
            shape((9, total + 2, low, cout), BF16),
        ),
        "main",
        [
            pltpu.VMEM(((total + 2) * low, cin), BF16),
            pltpu.VMEM((3, total + 2, ho + 2, wo, cout), BF16),
            pltpu.VMEM((cout, total * high), BF16),
            pltpu.VMEM((cin, total * low), BF16),
            pltpu.VMEM((chunk, cin, cout), F32),
            pltpu.VMEM((chunk, cout, cout), F32),
        ],
    )(*blocks, w1, w2)

    recv = swap(send, "dp", 1)
    own, *sends = call(
        pair_kernel,
        (shape((chunk, tall + short, cout), F32),)
        + tuple(shape((chunk, tall + short, cout), BF16) for _ in range(far_size - 1)),
        "pair",
    )(keep, recv)
    recvs = [swap(value, "dp", hop, 2) for hop, value in enumerate(sends, 1)]
    feature_grad = call(
        lambda *refs: input_grad_kernel(frames, *refs),
        shape((frames * low, cin), BF16),
        "input_grad",
    )(dbox, w1)
    factor = 1.0 / math.sqrt(clips * dp * total * high)
    share = call(
        lambda *refs: sum_kernel(factor, *refs), shape((chunk, tall + short, cout), BF16), "sum"
    )(own, *recvs)
    shares = [share] + [swap(share, "tm", hop) for hop in range(1, tm)]
    one, two = call(
        lambda *refs: spread_kernel(tall, *refs),
        (shape((taps, tall, cout), F32), shape((taps, short, cout), F32)),
        "spread",
    )(*shares)
    return (
        feature_grad.reshape(features.shape),
        one.reshape(3, 3, 3, tall, cout),
        two.reshape(3, 3, 3, short, cout),
    )


def solution(mesh):
    in_specs = (P("dp", "tm", None, None, None), P("dp", "tm", None, None, None), P(), P())
    out_specs = (
        P("dp", "tm", None, None, None),
        P(None, None, None, "dp", None),
        P(None, None, None, "dp", None),
    )
    return jax.shard_map(
        on_device, mesh=mesh, in_specs=in_specs, out_specs=out_specs, check_vma=False
    )
```

time: 163 us -> 48.1 us (0.30)
  waiting for transfers between devices: 120 us -> 15 us
  Pallas kernels: 0 us -> 17.1 us
  matrix products: 13.9 us -> 0 us
  between operations: 14.1 us -> 0.66 us
  starting transfers between devices: 7.71 us -> 12.4 us
  other arithmetic: 4 us -> 0 us
    reduce_scatter x2 -> x0, waiting for transfers between devices: 75.9 us -> none  [the longest x1 44 us: on_device(): lax.psum_scatter(totals[0], 'dp', scatter_dimension=3, tiled=True)]
    psum x1 -> x0, waiting for transfers between devices: 39.9 us -> none  [on_device(): totals = lax.psum((grad_first, grad_second), 'tm')]
    pallas_call x0 -> x6, Pallas kernels: none -> 17.1 us  [the longest x1 6.92 us: on_device(): call(main_body, (shape((far_size, chunk, tall + short, cout), F32), shape...]
    ppermute x3 -> x10, waiting for transfers between devices: 4.51 us -> 15 us  [swap(): lax.ppermute(value, axis, [(i, i ^ hop * stride) for i in range(size)])]
    conv_general_dilated x3 -> x0, matrix products: 10.3 us -> none  [the longest x2 8.03 us: kernel_grad(): lax.conv_general_dilated(padded, cotangent, (1, 1, 1), 'VALID', dimension...]
    ppermute x3 -> x10, starting transfers between devices: 7.59 us -> 12.4 us  [swap(): lax.ppermute(value, axis, [(i, i ^ hop * stride) for i in range(size)])]
    slice x2 -> x0, matrix products: 3.63 us -> none  [the longest x1 2.36 us: on_device(): back_all = data_grad(upstream, weight_two)[:, :, 1:-1, 1:-1]]
    mul x3 -> x0, other arithmetic: 3.53 us -> none  [the longest x2 3.46 us: on_device(): return (feature_grad, shares[0] * factor, shares[1] * factor)]
  transfers between devices with their start and end apart: 6 -> 10, of which waited for: 4 -> 7; matrix products, arithmetic and copies ran while one was open for 11% -> 0% of each run, Pallas kernels for 0% -> 6%
where the time goes in v1:
time: 48.1 us; the launch traced here: 47.8 us
  Pallas kernels  17.1 us (36%)
  waiting for transfers between devices  15 us (31%)
  starting transfers between devices  12.4 us (26%)
  local copies, waits for them, and re-layouts  2.67 us (6%)
  between operations  0.66 us (1%)
    ppermute x10, waiting for transfers between devices, swap(): lax.ppermute(value, axis, [(i, i ^ hop * stride) for i in range(size)])  15 us
    ppermute x10, starting transfers between devices, swap(): lax.ppermute(value, axis, [(i, i ^ hop * stride) for i in range(size)])  12.4 us
    pallas_call x1, Pallas kernels, on_device(): call(main_body, (shape((far_size, chunk, tall + short, cout), F32), shape...  6.92 us
    pallas_call x1, Pallas kernels, on_device(): call(lambda *refs: input_grad_kernel(frames, *refs), shape((frames * low,...  2.97 us
    unnamed x20, local copies, waits for them, and re-layouts  2.67 us
    pallas_call x1, Pallas kernels, on_device(): call(lambda *refs: spread_kernel(tall, *refs), (shape((taps, tall, cout),...  1.97 us
    pallas_call x1, Pallas kernels, on_device(): call(pair_kernel, (shape((chunk, tall + short, cout), F32),) + tuple((sha...  1.95 us
    pallas_call x1, Pallas kernels, on_device(): call(lambda *refs: sum_kernel(factor, *refs), shape((chunk, tall + short,...  1.72 us
  transfers between devices with their start and end apart: 10, of which 7 were waited for; matrix products, arithmetic and copies ran while one was open for 0% of the time, Pallas kernels for 6%

profile of v1, /device:TPU:0, one launch (start us, length us, event | category | flops | bytes accessed | tf_op | source)
XLA Modules:
  0.0 47.8 jit_solution(6046994112636999709)
XLA Ops:
  0.6 1.5 %pack.1.refs_0_ = bf16[4,96,128]{2,1,0:T(8,128)(2,1)} custom-call(bf16[4,16,256]{2,1,0:T(8,128)(2,1)} %bitcast.12, bf16[4,4,16,128]{3,2,1,0:T(8,128)(2,1)} %bitcast.10), custom_call_target="tpu_custom_call" | custom-call | tf_op jit(solution)/shard_map/pack/pallas_call | solution.py:214
  2.2 3.9 %collective-permute-start.2 = (bf16[4,96,128]{2,1,0:T(8,128)(2,1)}, bf16[4,96,128]{2,1,0:T(8,128)(2,1)S(1)}, u32[]{:S(2)}, u32[]{:S(2)}) collective-permute-start(bf16[4,96,128]{2,1,0:T(8,128)(2,1)} %pack.1.refs_0_), channel_id=1, source_target_pairs={{0,24},{8,16},{16,8},{24,0},{1,25},{9,17},{17,9},{25,1},{2,26},{10... | collective-permute-start | bytes 294920 | tf_op jit(solution)/shard_map/ppermute | solution.py:15
  6.1 0.5 %collective-permute-start.1 = (bf16[4,96,128]{2,1,0:T(8,128)(2,1)}, bf16[4,96,128]{2,1,0:T(8,128)(2,1)S(1)}, u32[]{:S(2)}, u32[]{:S(2)}) collective-permute-start(bf16[4,96,128]{2,1,0:T(8,128)(2,1)} %pack.1.refs_0_), channel_id=1, source_target_pairs={{0,16},{8,24},{16,0},{24,8},{1,17},{9,25},{17,1},{25,9},{2,18},{10... | collective-permute-start | bytes 294920 | tf_op jit(solution)/shard_map/ppermute | solution.py:15
  6.6 0.1 collective-permute-start
  6.6 2.9 %collective-permute-done.2.refs_3_ = bf16[4,96,128]{2,1,0:T(8,128)(2,1)S(1)} collective-permute-done((bf16[4,96,128]{2,1,0:T(8,128)(2,1)}, bf16[4,96,128]{2,1,0:T(8,128)(2,1)S(1)}, u32[]{:S(2)}, u32[]{:S(2)}) %collective-permute-start.2) | collective-permute-done | bytes 98336 | tf_op jit(solution)/shard_map/ppermute | solution.py:15
  9.5 0.0 copy-start.1
  9.6 1.6 %collective-permute-done.1.refs_2_ = bf16[4,96,128]{2,1,0:T(8,128)(2,1)S(1)} collective-permute-done((bf16[4,96,128]{2,1,0:T(8,128)(2,1)}, bf16[4,96,128]{2,1,0:T(8,128)(2,1)S(1)}, u32[]{:S(2)}, u32[]{:S(2)}) %collective-permute-start.1) | collective-permute-done | bytes 98336 | tf_op jit(solution)/shard_map/ppermute | solution.py:15
  11.2 0.0 copy-start.2
  11.2 0.3 collective-permute-done.refs_1_
  11.5 0.0 copy-start.3
  11.5 0.0 copy-done.1
  11.5 0.3 copy-done.2
  11.8 0.3 copy-done.3
  12.2 6.9 %main.1 = (f32[4,7,48,128]{3,2,1,0:T(8,128)}, bf16[4,7,48,128]{3,2,1,0:T(8,128)(2,1)}, bf16[9,18,16,128]{3,2,1,0:T(8,128)(2,1)}) custom-call(bf16[4,96,128]{2,1,0:T(8,128)(2,1)} %pack.1.refs_0_, bf16[4,96,128]{2,1,0:T(8,128)(2,1)} %copy-done.3, bf16[4,96,128]{2,1,0:T(8,128)(2,1)} %copy-done.2, bf16[4,96,128]{2,1,0:T(8,128)(2,1)} %copy-done.1, ...), custom_call_target="tpu_custom_call" | custom-call | tf_op jit(solution)/shard_map/main/pallas_call | solution.py:225
  19.1 0.0 collective-permute-start.3
  19.1 1.9 %collective-permute-done.3.recv_ref = bf16[4,7,48,128]{3,2,1,0:T(8,128)(2,1)S(1)} collective-permute-done((bf16[4,7,48,128]{3,2,1,0:T(8,128)(2,1)}, bf16[4,7,48,128]{3,2,1,0:T(8,128)(2,1)S(1)}, u32[]{:S(2)}, u32[]{:S(2)}) %collective-permute-start.3) | collective-permute-done | bytes 344096 | tf_op jit(solution)/shard_map/ppermute | solution.py:15
  20.9 0.0 copy-start
  21.0 0.7 %copy-done = bf16[4,7,48,128]{3,2,1,0:T(8,128)(2,1)} copy-done((bf16[4,7,48,128]{3,2,1,0:T(8,128)(2,1)}, bf16[4,7,48,128]{3,2,1,0:T(8,128)(2,1)S(1)}, u32[]{:S(2)}) %copy-start) | copy-done | bytes 344088
  21.7 2.0 %pair.1 = (f32[7,48,128]{2,1,0:T(8,128)}, bf16[7,48,128]{2,1,0:T(8,128)(2,1)}, bf16[7,48,128]{2,1,0:T(8,128)(2,1)}, bf16[7,48,128]{2,1,0:T(8,128)(2,1)}) custom-call(f32[4,7,48,128]{3,2,1,0:T(8,128)} %get-tuple-element.13.keep_ref, bf16[4,7,48,128]{3,2,1,0:T(8,128)(2,1)} %copy-done), custom_call_target="tpu_custom_call" | custom-call | tf_op jit(solution)/shard_map/pair/pallas_call | solution.py:244
  23.6 1.6 %collective-permute-start.4 = (bf16[7,48,128]{2,1,0:T(8,128)(2,1)}, bf16[7,48,128]{2,1,0:T(8,128)(2,1)S(1)}, u32[]{:S(2)}, u32[]{:S(2)}) collective-permute-start(bf16[7,48,128]{2,1,0:T(8,128)(2,1)} %get-tuple-element.16), channel_id=1, source_target_pairs={{0,2},{1,3},{2,0},{3,1},{4,6},{5,7},{6,4},{7,5},{8,10},{9,11},{10,... | collective-permute-start | bytes 258056 | tf_op jit(solution)/shard_map/ppermute | solution.py:15
  25.2 2.6 %collective-permute-start.5 = (bf16[7,48,128]{2,1,0:T(8,128)(2,1)}, bf16[7,48,128]{2,1,0:T(8,128)(2,1)S(1)}, u32[]{:S(2)}, u32[]{:S(2)}) collective-permute-start(bf16[7,48,128]{2,1,0:T(8,128)(2,1)} %get-tuple-element.17), channel_id=1, source_target_pairs={{0,4},{1,5},{2,6},{3,7},{4,0},{5,1},{6,2},{7,3},{8,12},{9,13},{10,... | collective-permute-start | bytes 258056 | tf_op jit(solution)/shard_map/ppermute | solution.py:15
  27.8 0.2 collective-permute-start.6
  28.0 0.4 collective-permute-done.4.refs_1_
  28.4 0.0 copy-start.7
  28.4 6.8 %collective-permute-done.5.refs_2_ = bf16[7,48,128]{2,1,0:T(8,128)(2,1)S(1)} collective-permute-done((bf16[7,48,128]{2,1,0:T(8,128)(2,1)}, bf16[7,48,128]{2,1,0:T(8,128)(2,1)S(1)}, u32[]{:S(2)}, u32[]{:S(2)}) %collective-permute-start.5) | collective-permute-done | bytes 86048 | tf_op jit(solution)/shard_map/ppermute | solution.py:15
  35.2 0.0 copy-start.8
  35.2 0.0 collective-permute-done.6.refs_3_
  35.2 0.0 copy-start.9
  35.2 0.0 copy-done.7
  35.2 0.6 %copy-done.8 = bf16[7,48,128]{2,1,0:T(8,128)(2,1)} copy-done((bf16[7,48,128]{2,1,0:T(8,128)(2,1)}, bf16[7,48,128]{2,1,0:T(8,128)(2,1)S(1)}, u32[]{:S(2)}) %copy-start.8) | copy-done | bytes 86040
  35.8 0.0 copy-done.9
  35.9 1.7 %sum.1.refs_0_ = bf16[7,48,128]{2,1,0:T(8,128)(2,1)} custom-call(f32[7,48,128]{2,1,0:T(8,128)} %get-tuple-element.15.refs_0_, bf16[7,48,128]{2,1,0:T(8,128)(2,1)} %copy-done.7, bf16[7,48,128]{2,1,0:T(8,128)(2,1)} %copy-done.8, bf16[7,48,128]{2,1,0:T(8,128)(2,1)} %copy-done.9), custom_call_target="tpu_custom_call" | custom-call | tf_op jit(solution)/shard_map/sum/pallas_call | solution.py:257
  37.6 1.6 %collective-permute-start.9 = (bf16[7,48,128]{2,1,0:T(8,128)(2,1)}, bf16[7,48,128]{2,1,0:T(8,128)(2,1)S(1)}, u32[]{:S(2)}, u32[]{:S(2)}) collective-permute-start(bf16[7,48,128]{2,1,0:T(8,128)(2,1)} %sum.1.refs_0_), channel_id=1, source_target_pairs={{0,24},{8,16},{16,8},{24,0},{1,25},{9,17},{17,9},{25,1},{2,26},{10... | collective-permute-start | bytes 258056 | tf_op jit(solution)/shard_map/ppermute | solution.py:15
  39.2 1.3 %collective-permute-start.8 = (bf16[7,48,128]{2,1,0:T(8,128)(2,1)}, bf16[7,48,128]{2,1,0:T(8,128)(2,1)S(1)}, u32[]{:S(2)}, u32[]{:S(2)}) collective-permute-start(bf16[7,48,128]{2,1,0:T(8,128)(2,1)} %sum.1.refs_0_), channel_id=1, source_target_pairs={{0,16},{8,24},{16,0},{24,8},{1,17},{9,25},{17,1},{25,9},{2,18},{10... | collective-permute-start | bytes 258056 | tf_op jit(solution)/shard_map/ppermute | solution.py:15
  40.5 0.6 %collective-permute-start.7 = (bf16[7,48,128]{2,1,0:T(8,128)(2,1)}, bf16[7,48,128]{2,1,0:T(8,128)(2,1)S(1)}, u32[]{:S(2)}, u32[]{:S(2)}) collective-permute-start(bf16[7,48,128]{2,1,0:T(8,128)(2,1)} %sum.1.refs_0_), channel_id=1, source_target_pairs={{0,8},{8,0},{16,24},{24,16},{1,9},{9,1},{17,25},{25,17},{2,10},{10... | collective-permute-start | bytes 258056 | tf_op jit(solution)/shard_map/ppermute | solution.py:15
  41.1 3.0 %input_grad.1 = bf16[64,256]{1,0:T(8,128)(2,1)} custom-call(bf16[9,18,16,128]{3,2,1,0:T(8,128)(2,1)} %get-tuple-element.12.refs_0_, bf16[27,256,128]{2,1,0:T(8,128)(2,1)} %bitcast.8), custom_call_target="tpu_custom_call" | custom-call | tf_op jit(solution)/shard_map/input_grad/pallas_call | solution.py:251
  44.0 0.0 collective-permute-done.9.refs_3_
  44.1 0.0 copy-start.4
  44.1 0.0 collective-permute-done.8.refs_2_
  44.1 0.0 copy-start.5
  44.1 1.1 %collective-permute-done.7.refs_1_ = bf16[7,48,128]{2,1,0:T(8,128)(2,1)S(1)} collective-permute-done((bf16[7,48,128]{2,1,0:T(8,128)(2,1)}, bf16[7,48,128]{2,1,0:T(8,128)(2,1)S(1)}, u32[]{:S(2)}, u32[]{:S(2)}) %collective-permute-start.7) | collective-permute-done | bytes 86048 | tf_op jit(solution)/shard_map/ppermute | solution.py:15
  45.2 0.0 copy-done.4
  45.2 0.0 copy-done.5
  45.2 0.0 copy-start.6
  45.2 0.6 %copy-done.6 = bf16[7,48,128]{2,1,0:T(8,128)(2,1)} copy-done((bf16[7,48,128]{2,1,0:T(8,128)(2,1)}, bf16[7,48,128]{2,1,0:T(8,128)(2,1)S(1)}, u32[]{:S(2)}) %copy-start.6) | copy-done | bytes 86040
  45.8 2.0 %spread.1 = (f32[27,32,128]{2,1,0:T(8,128)}, f32[27,16,128]{2,1,0:T(8,128)}) custom-call(bf16[7,48,128]{2,1,0:T(8,128)(2,1)} %sum.1.refs_0_, bf16[7,48,128]{2,1,0:T(8,128)(2,1)} %copy-done.6, bf16[7,48,128]{2,1,0:T(8,128)(2,1)} %copy-done.5, bf16[7,48,128]{2,1,0:T(8,128)(2,1)} %copy-done.4), custom_call_target="tpu_custom_call" | custom-call | tf_op jit(solution)/shard_map/spread/pallas_call | solution.py:261
Async XLA Ops:
  2.2 7.4 %collective-permute-start.2 = (bf16[4,96,128]{2,1,0:T(8,128)(2,1)}, bf16[4,96,128]{2,1,0:T(8,128)(2,1)S(1)}, u32[]{:S(2)}, u32[]{:S(2)}) collective-permute-start(bf16[4,96,128]{2,1,0:T(8,128)(2,1)} %pack.1.refs_0_), channel_id=1, source_target_pairs={{0,24},{8,16},{16,8},{24,0},{1,25},{9,17},{17,9},{25,1},{2,26},{10... | collective-permute-start | bytes 294920 | tf_op jit(solution)/shard_map/ppermute | solution.py:15
  6.1 5.1 %collective-permute-start.1 = (bf16[4,96,128]{2,1,0:T(8,128)(2,1)}, bf16[4,96,128]{2,1,0:T(8,128)(2,1)S(1)}, u32[]{:S(2)}, u32[]{:S(2)}) collective-permute-start(bf16[4,96,128]{2,1,0:T(8,128)(2,1)} %pack.1.refs_0_), channel_id=1, source_target_pairs={{0,16},{8,24},{16,0},{24,8},{1,17},{9,25},{17,1},{25,9},{2,18},{10... | collective-permute-start | bytes 294920 | tf_op jit(solution)/shard_map/ppermute | solution.py:15
  6.6 4.9 %collective-permute-start = (bf16[4,96,128]{2,1,0:T(8,128)(2,1)}, bf16[4,96,128]{2,1,0:T(8,128)(2,1)S(1)}, u32[]{:S(2)}, u32[]{:S(2)}) collective-permute-start(bf16[4,96,128]{2,1,0:T(8,128)(2,1)} %pack.1.refs_0_), channel_id=1, source_target_pairs={{0,8},{8,0},{16,24},{24,16},{1,9},{9,1},{17,25},{25,17},{2,10},{10... | collective-permute-start | bytes 294920 | tf_op jit(solution)/shard_map/ppermute | solution.py:15
  9.5 2.0 %copy-start.1 = (bf16[4,96,128]{2,1,0:T(8,128)(2,1)}, bf16[4,96,128]{2,1,0:T(8,128)(2,1)S(1)}, u32[]{:S(2)}) copy-start(bf16[4,96,128]{2,1,0:T(8,128)(2,1)S(1)} %collective-permute-done.2.refs_3_) | copy-start | bytes 294916
  11.2 0.6 %copy-start.2 = (bf16[4,96,128]{2,1,0:T(8,128)(2,1)}, bf16[4,96,128]{2,1,0:T(8,128)(2,1)S(1)}, u32[]{:S(2)}) copy-start(bf16[4,96,128]{2,1,0:T(8,128)(2,1)S(1)} %collective-permute-done.1.refs_2_) | copy-start | bytes 294916
  11.5 0.6 %copy-start.3 = (bf16[4,96,128]{2,1,0:T(8,128)(2,1)}, bf16[4,96,128]{2,1,0:T(8,128)(2,1)S(1)}, u32[]{:S(2)}) copy-start(bf16[4,96,128]{2,1,0:T(8,128)(2,1)S(1)} %collective-permute-done.refs_1_) | copy-start | bytes 294916
  19.1 1.9 %collective-permute-start.3 = (bf16[4,7,48,128]{3,2,1,0:T(8,128)(2,1)}, bf16[4,7,48,128]{3,2,1,0:T(8,128)(2,1)S(1)}, u32[]{:S(2)}, u32[]{:S(2)}) collective-permute-start(bf16[4,7,48,128]{3,2,1,0:T(8,128)(2,1)} %get-tuple-element.14), channel_id=1, source_target_pairs={{0,1},{1,0},{2,3},{3,2},{4,5},{5,4},{6,7},{7,6},{8,9},{9,8},{10,11... | collective-permute-start | bytes 1032200 | tf_op jit(solution)/shard_map/ppermute | solution.py:15
  20.9 0.7 %copy-start = (bf16[4,7,48,128]{3,2,1,0:T(8,128)(2,1)}, bf16[4,7,48,128]{3,2,1,0:T(8,128)(2,1)S(1)}, u32[]{:S(2)}) copy-start(bf16[4,7,48,128]{3,2,1,0:T(8,128)(2,1)S(1)} %collective-permute-done.3.recv_ref) | copy-start | bytes 1032196
  23.6 4.8 %collective-permute-start.4 = (bf16[7,48,128]{2,1,0:T(8,128)(2,1)}, bf16[7,48,128]{2,1,0:T(8,128)(2,1)S(1)}, u32[]{:S(2)}, u32[]{:S(2)}) collective-permute-start(bf16[7,48,128]{2,1,0:T(8,128)(2,1)} %get-tuple-element.16), channel_id=1, source_target_pairs={{0,2},{1,3},{2,0},{3,1},{4,6},{5,7},{6,4},{7,5},{8,10},{9,11},{10,... | collective-permute-start | bytes 258056 | tf_op jit(solution)/shard_map/ppermute | solution.py:15
  25.2 10.0 %collective-permute-start.5 = (bf16[7,48,128]{2,1,0:T(8,128)(2,1)}, bf16[7,48,128]{2,1,0:T(8,128)(2,1)S(1)}, u32[]{:S(2)}, u32[]{:S(2)}) collective-permute-start(bf16[7,48,128]{2,1,0:T(8,128)(2,1)} %get-tuple-element.17), channel_id=1, source_target_pairs={{0,4},{1,5},{2,6},{3,7},{4,0},{5,1},{6,2},{7,3},{8,12},{9,13},{10,... | collective-permute-start | bytes 258056 | tf_op jit(solution)/shard_map/ppermute | solution.py:15
  27.8 7.4 %collective-permute-start.6 = (bf16[7,48,128]{2,1,0:T(8,128)(2,1)}, bf16[7,48,128]{2,1,0:T(8,128)(2,1)S(1)}, u32[]{:S(2)}, u32[]{:S(2)}) collective-permute-start(bf16[7,48,128]{2,1,0:T(8,128)(2,1)} %get-tuple-element.18), channel_id=1, source_target_pairs={{0,6},{1,7},{2,4},{3,5},{4,2},{5,3},{6,0},{7,1},{8,14},{9,15},{10,... | collective-permute-start | bytes 258056 | tf_op jit(solution)/shard_map/ppermute | solution.py:15
  28.4 6.8 %copy-start.7 = (bf16[7,48,128]{2,1,0:T(8,128)(2,1)}, bf16[7,48,128]{2,1,0:T(8,128)(2,1)S(1)}, u32[]{:S(2)}) copy-start(bf16[7,48,128]{2,1,0:T(8,128)(2,1)S(1)} %collective-permute-done.4.refs_1_) | copy-start | bytes 258052
  35.2 0.6 %copy-start.8 = (bf16[7,48,128]{2,1,0:T(8,128)(2,1)}, bf16[7,48,128]{2,1,0:T(8,128)(2,1)S(1)}, u32[]{:S(2)}) copy-start(bf16[7,48,128]{2,1,0:T(8,128)(2,1)S(1)} %collective-permute-done.5.refs_2_) | copy-start | bytes 258052
  35.2 0.7 %copy-start.9 = (bf16[7,48,128]{2,1,0:T(8,128)(2,1)}, bf16[7,48,128]{2,1,0:T(8,128)(2,1)S(1)}, u32[]{:S(2)}) copy-start(bf16[7,48,128]{2,1,0:T(8,128)(2,1)S(1)} %collective-permute-done.6.refs_3_) | copy-start | bytes 258052
  37.6 6.5 %collective-permute-start.9 = (bf16[7,48,128]{2,1,0:T(8,128)(2,1)}, bf16[7,48,128]{2,1,0:T(8,128)(2,1)S(1)}, u32[]{:S(2)}, u32[]{:S(2)}) collective-permute-start(bf16[7,48,128]{2,1,0:T(8,128)(2,1)} %sum.1.refs_0_), channel_id=1, source_target_pairs={{0,24},{8,16},{16,8},{24,0},{1,25},{9,17},{17,9},{25,1},{2,26},{10... | collective-permute-start | bytes 258056 | tf_op jit(solution)/shard_map/ppermute | solution.py:15
  39.2 4.9 %collective-permute-start.8 = (bf16[7,48,128]{2,1,0:T(8,128)(2,1)}, bf16[7,48,128]{2,1,0:T(8,128)(2,1)S(1)}, u32[]{:S(2)}, u32[]{:S(2)}) collective-permute-start(bf16[7,48,128]{2,1,0:T(8,128)(2,1)} %sum.1.refs_0_), channel_id=1, source_target_pairs={{0,16},{8,24},{16,0},{24,8},{1,17},{9,25},{17,1},{25,9},{2,18},{10... | collective-permute-start | bytes 258056 | tf_op jit(solution)/shard_map/ppermute | solution.py:15
  40.5 4.7 %collective-permute-start.7 = (bf16[7,48,128]{2,1,0:T(8,128)(2,1)}, bf16[7,48,128]{2,1,0:T(8,128)(2,1)S(1)}, u32[]{:S(2)}, u32[]{:S(2)}) collective-permute-start(bf16[7,48,128]{2,1,0:T(8,128)(2,1)} %sum.1.refs_0_), channel_id=1, source_target_pairs={{0,8},{8,0},{16,24},{24,16},{1,9},{9,1},{17,25},{25,17},{2,10},{10... | collective-permute-start | bytes 258056 | tf_op jit(solution)/shard_map/ppermute | solution.py:15
  44.1 1.1 %copy-start.4 = (bf16[7,48,128]{2,1,0:T(8,128)(2,1)}, bf16[7,48,128]{2,1,0:T(8,128)(2,1)S(1)}, u32[]{:S(2)}) copy-start(bf16[7,48,128]{2,1,0:T(8,128)(2,1)S(1)} %collective-permute-done.9.refs_3_) | copy-start | bytes 258052
  44.1 1.1 %copy-start.5 = (bf16[7,48,128]{2,1,0:T(8,128)(2,1)}, bf16[7,48,128]{2,1,0:T(8,128)(2,1)S(1)}, u32[]{:S(2)}) copy-start(bf16[7,48,128]{2,1,0:T(8,128)(2,1)S(1)} %collective-permute-done.8.refs_2_) | copy-start | bytes 258052
  45.2 0.6 %copy-start.6 = (bf16[7,48,128]{2,1,0:T(8,128)(2,1)}, bf16[7,48,128]{2,1,0:T(8,128)(2,1)S(1)}, u32[]{:S(2)}) copy-start(bf16[7,48,128]{2,1,0:T(8,128)(2,1)S(1)} %collective-permute-done.7.refs_1_) | copy-start | bytes 258052

commit v2 on v1

--- a/solution.py
+++ b/solution.py
@@ -15,14 +15,15 @@
     return lax.ppermute(value, axis, [(i, i ^ (hop * stride)) for i in range(size)])
 
 
-def call(body, out_shape, name, scratch=(), flops=0):
-    return pl.pallas_call(
+def call(body, out_shape, name, scratch=(), grant=8):
+    kernel = pl.pallas_call(
         body,
         out_shape=out_shape,
         scratch_shapes=list(scratch),
         name=name,
-        cost_estimate=pl.CostEstimate(flops=flops, transcendentals=0, bytes_accessed=0) if flops else None,
-    )
+        compiler_params=pltpu.CompilerParams(vmem_limit_bytes=grant << 20),
+    )
+    return lambda *values: kernel(*(pltpu.with_memory_space_constraint(v, pltpu.VMEM) for v in values))
 
 
 def rows_of(value):
@@ -207,13 +208,13 @@
     low, high = hi * wi, ho * wo
     far_size = dp // 2
     tall, short = cin // dp, cout // dp
-    shape = jax.ShapeDtypeStruct
+    shape, near = jax.ShapeDtypeStruct, pltpu.VMEM
     w1 = weight_one.reshape(taps, cin, cout)
     w2 = weight_two.reshape(taps, cout, cout)
 
     packed = call(
         pack_kernel,
-        shape((frames, low * (cin // cout) + high, cout), BF16),
+        near((frames, low * (cin // cout) + high, cout), BF16),
         "pack",
         [pltpu.VMEM((frames * ho, wo, cout), F32)],
     )(features.reshape(frames, low, cin), upstream.reshape(frames, ho, wo, cout))
@@ -225,9 +226,9 @@
     keep, send, dbox = call(
         main_body,
         (
-            shape((far_size, chunk, tall + short, cout), F32),
-            shape((far_size, chunk, tall + short, cout), BF16),
-            shape((9, total + 2, low, cout), BF16),
+            near((far_size, chunk, tall + short, cout), F32),
+            near((far_size, chunk, tall + short, cout), BF16),
+            near((9, total + 2, low, cout), BF16),
         ),
         "main",
         [
@@ -238,13 +239,14 @@
             pltpu.VMEM((chunk, cin, cout), F32),
             pltpu.VMEM((chunk, cout, cout), F32),
         ],
+        grant=32,
     )(*blocks, w1, w2)
 
     recv = swap(send, "dp", 1)
     own, *sends = call(
         pair_kernel,
-        (shape((chunk, tall + short, cout), F32),)
-        + tuple(shape((chunk, tall + short, cout), BF16) for _ in range(far_size - 1)),
+        (near((chunk, tall + short, cout), F32),)
+        + tuple(near((chunk, tall + short, cout), BF16) for _ in range(far_size - 1)),
         "pair",
     )(keep, recv)
     recvs = [swap(value, "dp", hop, 2) for hop, value in enumerate(sends, 1)]
@@ -255,7 +257,7 @@
     )(dbox, w1)
     factor = 1.0 / math.sqrt(clips * dp * total * high)
     share = call(
-        lambda *refs: sum_kernel(factor, *refs), shape((chunk, tall + short, cout), BF16), "sum"
+        lambda *refs: sum_kernel(factor, *refs), near((chunk, tall + short, cout), BF16), "sum"
     )(own, *recvs)
     shares = [share] + [swap(share, "tm", hop) for hop in range(1, tm)]
     one, two = call(

time: 48.1 us -> 39.9 us (0.83)
  Pallas kernels: 17.1 us -> 6.21 us
  local copies, waits for them, and re-layouts: 2.67 us -> 4.23 us
  waiting for transfers between devices: 15 us -> 15.8 us
    pallas_call x6, Pallas kernels: 17.1 us -> 6.21 us  [call(): kernel(*(pltpu.with_memory_space_constraint(v, pltpu.VMEM) for v in values))]
    unnamed x20 -> x8, local copies, waits for them, and re-layouts: 2.67 us -> 4.23 us
    ppermute x10, waiting for transfers between devices: 15 us -> 15.8 us  [swap(): lax.ppermute(value, axis, [(i, i ^ hop * stride) for i in range(size)])]
  transfers between devices with their start and end apart: 10 -> 10, of which waited for: 7 -> 9; matrix products, arithmetic and copies ran while one was open for 0% -> 0% of each run, Pallas kernels for 6% -> 3%
where the time goes in v2:
time: 39.9 us; the launch traced here: 39.6 us
  waiting for transfers between devices  15.8 us (40%)
  starting transfers between devices  12.7 us (32%)
  Pallas kernels  6.21 us (16%)
  local copies, waits for them, and re-layouts  4.23 us (11%)
  between operations  0.68 us (2%)
    ppermute x10, waiting for transfers between devices, swap(): lax.ppermute(value, axis, [(i, i ^ hop * stride) for i in range(size)])  15.8 us
    ppermute x10, starting transfers between devices, swap(): lax.ppermute(value, axis, [(i, i ^ hop * stride) for i in range(size)])  12.7 us
    pallas_call x6, Pallas kernels, call(): kernel(*(pltpu.with_memory_space_constraint(v, pltpu.VMEM) for v in values))  6.21 us
    unnamed x8, local copies, waits for them, and re-layouts  4.23 us
  transfers between devices with their start and end apart: 10, of which 9 were waited for; matrix products, arithmetic and copies ran while one was open for 0% of the time, Pallas kernels for 3%

profile of v2, /device:TPU:0, one launch (start us, length us, event | category | flops | bytes accessed | tf_op | source)
XLA Modules:
  0.0 39.6 jit_solution(5162965030541705918)
XLA Ops:
  0.6 0.0 copy-start.2
  0.6 0.8 %copy-done.2 = bf16[1,4,4,16,128]{4,3,2,1,0:T(8,128)(2,1)S(1)} copy-done((bf16[1,4,4,16,128]{4,3,2,1,0:T(8,128)(2,1)S(1)}, bf16[1,4,4,16,128]{4,3,2,1,0:T(8,128)(2,1)}, u32[]{:S(2)}) %copy-start.2) | copy-done | bytes 65560
  1.5 0.0 copy-start.3
  1.5 0.8 %copy-done.3 = bf16[1,4,2,8,256]{4,3,2,1,0:T(8,128)(2,1)S(1)} copy-done((bf16[1,4,2,8,256]{4,3,2,1,0:T(8,128)(2,1)S(1)}, bf16[1,4,2,8,256]{4,3,2,1,0:T(8,128)(2,1)}, u32[]{:S(2)}) %copy-start.3) | copy-done | bytes 32792
  2.3 4.0 %collective-permute-start.2 = (bf16[4,96,128]{2,1,0:T(8,128)(2,1)S(1)}, bf16[4,96,128]{2,1,0:T(8,128)(2,1)S(1)}, u32[]{:S(2)}, u32[]{:S(2)}) collective-permute-start(bf16[4,96,128]{2,1,0:T(8,128)(2,1)S(1)} %pack.1.refs_0_), channel_id=1, source_target_pairs={{0,24},{8,16},{16,8},{24,0},{1,25},{9,17},{17,9},{25,1},{2,26},{10... | collective-permute-start | bytes 294920 | tf_op jit(solution)/shard_map/ppermute | solution.py:15
  6.2 0.5 %collective-permute-start.1 = (bf16[4,96,128]{2,1,0:T(8,128)(2,1)S(1)}, bf16[4,96,128]{2,1,0:T(8,128)(2,1)S(1)}, u32[]{:S(2)}, u32[]{:S(2)}) collective-permute-start(bf16[4,96,128]{2,1,0:T(8,128)(2,1)S(1)} %pack.1.refs_0_), channel_id=1, source_target_pairs={{0,16},{8,24},{16,0},{24,8},{1,17},{9,25},{17,1},{25,9},{2,18},{10... | collective-permute-start | bytes 294920 | tf_op jit(solution)/shard_map/ppermute | solution.py:15
  6.8 0.1 collective-permute-start
  6.9 2.5 %collective-permute-done.2.refs_3_ = bf16[4,96,128]{2,1,0:T(8,128)(2,1)S(1)} collective-permute-done((bf16[4,96,128]{2,1,0:T(8,128)(2,1)S(1)}, bf16[4,96,128]{2,1,0:T(8,128)(2,1)S(1)}, u32[]{:S(2)}, u32[]{:S(2)}) %collective-permute-start.2) | collective-permute-done | bytes 98336 | tf_op jit(solution)/shard_map/ppermute | solution.py:15
  9.4 1.7 %collective-permute-done.1.refs_2_ = bf16[4,96,128]{2,1,0:T(8,128)(2,1)S(1)} collective-permute-done((bf16[4,96,128]{2,1,0:T(8,128)(2,1)S(1)}, bf16[4,96,128]{2,1,0:T(8,128)(2,1)S(1)}, u32[]{:S(2)}, u32[]{:S(2)}) %collective-permute-start.1) | collective-permute-done | bytes 98336 | tf_op jit(solution)/shard_map/ppermute | solution.py:15
  11.1 0.3 collective-permute-done.refs_1_
  11.5 0.0 copy-start
  11.5 1.5 %copy-done = bf16[3,3,3,256,128]{4,3,2,1,0:T(8,128)(2,1)S(1)} copy-done((bf16[3,3,3,256,128]{4,3,2,1,0:T(8,128)(2,1)S(1)}, bf16[3,3,3,256,128]{4,3,2,1,0:T(8,128)(2,1)}, u32[]{:S(2)}) %copy-start) | copy-done | bytes 1769496
  13.0 0.0 copy-start.1
  13.0 1.2 %copy-done.1 = bf16[3,3,3,128,128]{4,3,2,1,0:T(8,128)(2,1)S(1)} copy-done((bf16[3,3,3,128,128]{4,3,2,1,0:T(8,128)(2,1)S(1)}, bf16[3,3,3,128,128]{4,3,2,1,0:T(8,128)(2,1)}, u32[]{:S(2)}) %copy-start.1) | copy-done | bytes 884760
  14.1 3.8 %main.1 = (f32[4,7,48,128]{3,2,1,0:T(8,128)S(1)}, bf16[4,7,48,128]{3,2,1,0:T(8,128)(2,1)S(1)}, bf16[9,18,16,128]{3,2,1,0:T(8,128)(2,1)S(1)}) custom-call(bf16[4,96,128]{2,1,0:T(8,128)(2,1)S(1)} %pack.1.refs_0_, bf16[4,96,128]{2,1,0:T(8,128)(2,1)S(1)} %collective-permute-done.refs_1_, bf16[4,96,128]{2,1,0:T(8,128)(2,1)S(1)} %collective-permute-done.1.refs_2_, ...), custom_call_target="tpu_custom_call" | custom-call | tf_op jit(solution)/shard_map/main/pallas_call | solution.py:26
  18.0 0.1 collective-permute-start.3
  18.0 1.6 %collective-permute-done.3.recv_ref = bf16[4,7,48,128]{3,2,1,0:T(8,128)(2,1)S(1)} collective-permute-done((bf16[4,7,48,128]{3,2,1,0:T(8,128)(2,1)S(1)}, bf16[4,7,48,128]{3,2,1,0:T(8,128)(2,1)S(1)}, u32[]{:S(2)}, u32[]{:S(2)}) %collective-permute-start.3) | collective-permute-done | bytes 344096 | tf_op jit(solution)/shard_map/ppermute | solution.py:15
  19.7 0.1 pair.1
  19.7 1.6 %collective-permute-start.4 = (bf16[7,48,128]{2,1,0:T(8,128)(2,1)S(1)}, bf16[7,48,128]{2,1,0:T(8,128)(2,1)S(1)}, u32[]{:S(2)}, u32[]{:S(2)}) collective-permute-start(bf16[7,48,128]{2,1,0:T(8,128)(2,1)S(1)} %get-tuple-element.16), channel_id=1, source_target_pairs={{0,2},{1,3},{2,0},{3,1},{4,6},{5,7},{6,4},{7,5},{8,10},{9,11},{10,... | collective-permute-start | bytes 258056 | tf_op jit(solution)/shard_map/ppermute | solution.py:15
  21.4 2.6 %collective-permute-start.5 = (bf16[7,48,128]{2,1,0:T(8,128)(2,1)S(1)}, bf16[7,48,128]{2,1,0:T(8,128)(2,1)S(1)}, u32[]{:S(2)}, u32[]{:S(2)}) collective-permute-start(bf16[7,48,128]{2,1,0:T(8,128)(2,1)S(1)} %get-tuple-element.17), channel_id=1, source_target_pairs={{0,4},{1,5},{2,6},{3,7},{4,0},{5,1},{6,2},{7,3},{8,12},{9,13},{10,... | collective-permute-start | bytes 258056 | tf_op jit(solution)/shard_map/ppermute | solution.py:15
  24.0 0.2 collective-permute-start.6
  24.2 0.2 collective-permute-done.4.refs_1_
  24.4 6.8 %collective-permute-done.5.refs_2_ = bf16[7,48,128]{2,1,0:T(8,128)(2,1)S(1)} collective-permute-done((bf16[7,48,128]{2,1,0:T(8,128)(2,1)S(1)}, bf16[7,48,128]{2,1,0:T(8,128)(2,1)S(1)}, u32[]{:S(2)}, u32[]{:S(2)}) %collective-permute-start.5) | collective-permute-done | bytes 86048 | tf_op jit(solution)/shard_map/ppermute | solution.py:15
  31.1 0.0 collective-permute-done.6.refs_3_
  31.2 0.1 sum.1.refs_0_
  31.2 1.7 %collective-permute-start.9 = (bf16[7,48,128]{2,1,0:T(8,128)(2,1)S(1)}, bf16[7,48,128]{2,1,0:T(8,128)(2,1)S(1)}, u32[]{:S(2)}, u32[]{:S(2)}) collective-permute-start(bf16[7,48,128]{2,1,0:T(8,128)(2,1)S(1)} %sum.1.refs_0_), channel_id=1, source_target_pairs={{0,24},{8,16},{16,8},{24,0},{1,25},{9,17},{17,9},{25,1},{2,26},{10... | collective-permute-start | bytes 258056 | tf_op jit(solution)/shard_map/ppermute | solution.py:15
  32.9 1.3 %collective-permute-start.8 = (bf16[7,48,128]{2,1,0:T(8,128)(2,1)S(1)}, bf16[7,48,128]{2,1,0:T(8,128)(2,1)S(1)}, u32[]{:S(2)}, u32[]{:S(2)}) collective-permute-start(bf16[7,48,128]{2,1,0:T(8,128)(2,1)S(1)} %sum.1.refs_0_), channel_id=1, source_target_pairs={{0,16},{8,24},{16,0},{24,8},{1,17},{9,25},{17,1},{25,9},{2,18},{10... | collective-permute-start | bytes 258056 | tf_op jit(solution)/shard_map/ppermute | solution.py:15
  34.2 0.6 %collective-permute-start.7 = (bf16[7,48,128]{2,1,0:T(8,128)(2,1)S(1)}, bf16[7,48,128]{2,1,0:T(8,128)(2,1)S(1)}, u32[]{:S(2)}, u32[]{:S(2)}) collective-permute-start(bf16[7,48,128]{2,1,0:T(8,128)(2,1)S(1)} %sum.1.refs_0_), channel_id=1, source_target_pairs={{0,8},{8,0},{16,24},{24,16},{1,9},{9,1},{17,25},{25,17},{2,10},{10... | collective-permute-start | bytes 258056 | tf_op jit(solution)/shard_map/ppermute | solution.py:15
  34.8 1.3 %input_grad.1 = bf16[64,256]{1,0:T(8,128)(2,1)} custom-call(bf16[9,18,16,128]{3,2,1,0:T(8,128)(2,1)S(1)} %get-tuple-element.12.refs_0_, bf16[27,256,128]{2,1,0:T(8,128)(2,1)S(1)} %bitcast.8), custom_call_target="tpu_custom_call" | custom-call | tf_op jit(solution)/shard_map/input_grad/pallas_call | solution.py:26
  36.0 0.6 %collective-permute-done.9.refs_3_ = bf16[7,48,128]{2,1,0:T(8,128)(2,1)S(1)} collective-permute-done((bf16[7,48,128]{2,1,0:T(8,128)(2,1)S(1)}, bf16[7,48,128]{2,1,0:T(8,128)(2,1)S(1)}, u32[]{:S(2)}, u32[]{:S(2)}) %collective-permute-start.9) | collective-permute-done | bytes 86048 | tf_op jit(solution)/shard_map/ppermute | solution.py:15
  36.7 0.9 %collective-permute-done.8.refs_2_ = bf16[7,48,128]{2,1,0:T(8,128)(2,1)S(1)} collective-permute-done((bf16[7,48,128]{2,1,0:T(8,128)(2,1)S(1)}, bf16[7,48,128]{2,1,0:T(8,128)(2,1)S(1)}, u32[]{:S(2)}, u32[]{:S(2)}) %collective-permute-start.8) | collective-permute-done | bytes 86048 | tf_op jit(solution)/shard_map/ppermute | solution.py:15
  37.6 1.1 %collective-permute-done.7.refs_1_ = bf16[7,48,128]{2,1,0:T(8,128)(2,1)S(1)} collective-permute-done((bf16[7,48,128]{2,1,0:T(8,128)(2,1)S(1)}, bf16[7,48,128]{2,1,0:T(8,128)(2,1)S(1)}, u32[]{:S(2)}, u32[]{:S(2)}) %collective-permute-start.7) | collective-permute-done | bytes 86048 | tf_op jit(solution)/shard_map/ppermute | solution.py:15
  38.7 1.0 %spread.1 = (f32[27,32,128]{2,1,0:T(8,128)}, f32[27,16,128]{2,1,0:T(8,128)}) custom-call(bf16[7,48,128]{2,1,0:T(8,128)(2,1)S(1)} %sum.1.refs_0_, bf16[7,48,128]{2,1,0:T(8,128)(2,1)S(1)} %collective-permute-done.7.refs_1_, bf16[7,48,128]{2,1,0:T(8,128)(2,1)S(1)} %collective-permute-done.8.refs_2_, bf16[7,48,128]{2,1,0:T(8,128)(2,1)S(1)} %collective-permute-done.9.refs_3_), custom_call_target="tpu_custom_call" | custom-call | tf_op jit(solution)/shard_map/spread/pallas_call | solution.py:26
  (1 shorter events, 0.0 us)
Async XLA Ops:
  0.6 0.8 %copy-start.2 = (bf16[1,4,4,16,128]{4,3,2,1,0:T(8,128)(2,1)S(1)}, bf16[1,4,4,16,128]{4,3,2,1,0:T(8,128)(2,1)}, u32[]{:S(2)}) copy-start(bf16[1,4,4,16,128]{4,3,2,1,0:T(8,128)(2,1)} %param.5) | copy-start | bytes 196612
  1.5 0.8 %copy-start.3 = (bf16[1,4,2,8,256]{4,3,2,1,0:T(8,128)(2,1)S(1)}, bf16[1,4,2,8,256]{4,3,2,1,0:T(8,128)(2,1)}, u32[]{:S(2)}) copy-start(bf16[1,4,2,8,256]{4,3,2,1,0:T(8,128)(2,1)} %param.4) | copy-start | bytes 98308
  2.3 7.2 %collective-permute-start.2 = (bf16[4,96,128]{2,1,0:T(8,128)(2,1)S(1)}, bf16[4,96,128]{2,1,0:T(8,128)(2,1)S(1)}, u32[]{:S(2)}, u32[]{:S(2)}) collective-permute-start(bf16[4,96,128]{2,1,0:T(8,128)(2,1)S(1)} %pack.1.refs_0_), channel_id=1, source_target_pairs={{0,24},{8,16},{16,8},{24,0},{1,25},{9,17},{17,9},{25,1},{2,26},{10... | collective-permute-start | bytes 294920 | tf_op jit(solution)/shard_map/ppermute | solution.py:15
  6.2 4.9 %collective-permute-start.1 = (bf16[4,96,128]{2,1,0:T(8,128)(2,1)S(1)}, bf16[4,96,128]{2,1,0:T(8,128)(2,1)S(1)}, u32[]{:S(2)}, u32[]{:S(2)}) collective-permute-start(bf16[4,96,128]{2,1,0:T(8,128)(2,1)S(1)} %pack.1.refs_0_), channel_id=1, source_target_pairs={{0,16},{8,24},{16,0},{24,8},{1,17},{9,25},{17,1},{25,9},{2,18},{10... | collective-permute-start | bytes 294920 | tf_op jit(solution)/shard_map/ppermute | solution.py:15
  6.8 4.7 %collective-permute-start = (bf16[4,96,128]{2,1,0:T(8,128)(2,1)S(1)}, bf16[4,96,128]{2,1,0:T(8,128)(2,1)S(1)}, u32[]{:S(2)}, u32[]{:S(2)}) collective-permute-start(bf16[4,96,128]{2,1,0:T(8,128)(2,1)S(1)} %pack.1.refs_0_), channel_id=1, source_target_pairs={{0,8},{8,0},{16,24},{24,16},{1,9},{9,1},{17,25},{25,17},{2,10},{10... | collective-permute-start | bytes 294920 | tf_op jit(solution)/shard_map/ppermute | solution.py:15
  11.5 1.5 %copy-start = (bf16[3,3,3,256,128]{4,3,2,1,0:T(8,128)(2,1)S(1)}, bf16[3,3,3,256,128]{4,3,2,1,0:T(8,128)(2,1)}, u32[]{:S(2)}) copy-start(bf16[3,3,3,256,128]{4,3,2,1,0:T(8,128)(2,1)} %param.6) | copy-start | bytes 5308420
  13.0 1.2 %copy-start.1 = (bf16[3,3,3,128,128]{4,3,2,1,0:T(8,128)(2,1)S(1)}, bf16[3,3,3,128,128]{4,3,2,1,0:T(8,128)(2,1)}, u32[]{:S(2)}) copy-start(bf16[3,3,3,128,128]{4,3,2,1,0:T(8,128)(2,1)} %param.7) | copy-start | bytes 2654212
  18.0 1.7 %collective-permute-start.3 = (bf16[4,7,48,128]{3,2,1,0:T(8,128)(2,1)S(1)}, bf16[4,7,48,128]{3,2,1,0:T(8,128)(2,1)S(1)}, u32[]{:S(2)}, u32[]{:S(2)}) collective-permute-start(bf16[4,7,48,128]{3,2,1,0:T(8,128)(2,1)S(1)} %get-tuple-element.14), channel_id=1, source_target_pairs={{0,1},{1,0},{2,3},{3,2},{4,5},{5,4},{6,7},{7,6},{8,9},{9,8},{10,11... | collective-permute-start | bytes 1032200 | tf_op jit(solution)/shard_map/ppermute | solution.py:15
  19.7 4.6 %collective-permute-start.4 = (bf16[7,48,128]{2,1,0:T(8,128)(2,1)S(1)}, bf16[7,48,128]{2,1,0:T(8,128)(2,1)S(1)}, u32[]{:S(2)}, u32[]{:S(2)}) collective-permute-start(bf16[7,48,128]{2,1,0:T(8,128)(2,1)S(1)} %get-tuple-element.16), channel_id=1, source_target_pairs={{0,2},{1,3},{2,0},{3,1},{4,6},{5,7},{6,4},{7,5},{8,10},{9,11},{10,... | collective-permute-start | bytes 258056 | tf_op jit(solution)/shard_map/ppermute | solution.py:15
  21.4 9.8 %collective-permute-start.5 = (bf16[7,48,128]{2,1,0:T(8,128)(2,1)S(1)}, bf16[7,48,128]{2,1,0:T(8,128)(2,1)S(1)}, u32[]{:S(2)}, u32[]{:S(2)}) collective-permute-start(bf16[7,48,128]{2,1,0:T(8,128)(2,1)S(1)} %get-tuple-element.17), channel_id=1, source_target_pairs={{0,4},{1,5},{2,6},{3,7},{4,0},{5,1},{6,2},{7,3},{8,12},{9,13},{10,... | collective-permute-start | bytes 258056 | tf_op jit(solution)/shard_map/ppermute | solution.py:15
  24.0 7.2 %collective-permute-start.6 = (bf16[7,48,128]{2,1,0:T(8,128)(2,1)S(1)}, bf16[7,48,128]{2,1,0:T(8,128)(2,1)S(1)}, u32[]{:S(2)}, u32[]{:S(2)}) collective-permute-start(bf16[7,48,128]{2,1,0:T(8,128)(2,1)S(1)} %get-tuple-element.18), channel_id=1, source_target_pairs={{0,6},{1,7},{2,4},{3,5},{4,2},{5,3},{6,0},{7,1},{8,14},{9,15},{10,... | collective-permute-start | bytes 258056 | tf_op jit(solution)/shard_map/ppermute | solution.py:15
  31.2 5.5 %collective-permute-start.9 = (bf16[7,48,128]{2,1,0:T(8,128)(2,1)S(1)}, bf16[7,48,128]{2,1,0:T(8,128)(2,1)S(1)}, u32[]{:S(2)}, u32[]{:S(2)}) collective-permute-start(bf16[7,48,128]{2,1,0:T(8,128)(2,1)S(1)} %sum.1.refs_0_), channel_id=1, source_target_pairs={{0,24},{8,16},{16,8},{24,0},{1,25},{9,17},{17,9},{25,1},{2,26},{10... | collective-permute-start | bytes 258056 | tf_op jit(solution)/shard_map/ppermute | solution.py:15
  32.9 4.7 %collective-permute-start.8 = (bf16[7,48,128]{2,1,0:T(8,128)(2,1)S(1)}, bf16[7,48,128]{2,1,0:T(8,128)(2,1)S(1)}, u32[]{:S(2)}, u32[]{:S(2)}) collective-permute-start(bf16[7,48,128]{2,1,0:T(8,128)(2,1)S(1)} %sum.1.refs_0_), channel_id=1, source_target_pairs={{0,16},{8,24},{16,0},{24,8},{1,17},{9,25},{17,1},{25,9},{2,18},{10... | collective-permute-start | bytes 258056 | tf_op jit(solution)/shard_map/ppermute | solution.py:15
  34.2 4.5 %collective-permute-start.7 = (bf16[7,48,128]{2,1,0:T(8,128)(2,1)S(1)}, bf16[7,48,128]{2,1,0:T(8,128)(2,1)S(1)}, u32[]{:S(2)}, u32[]{:S(2)}) collective-permute-start(bf16[7,48,128]{2,1,0:T(8,128)(2,1)S(1)} %sum.1.refs_0_), channel_id=1, source_target_pairs={{0,8},{8,0},{16,24},{24,16},{1,9},{9,1},{17,25},{25,17},{2,10},{10... | collective-permute-start | bytes 258056 | tf_op jit(solution)/shard_map/ppermute | solution.py:15

commit v3 on v2

--- a/solution.py
+++ b/solution.py
@@ -7,6 +7,7 @@
 from jax.experimental.pallas import tpu as pltpu
 from jax.sharding import PartitionSpec as P
 
+
 F32, BF16 = jnp.float32, jnp.bfloat16
 
 
@@ -15,15 +16,17 @@
     return lax.ppermute(value, axis, [(i, i ^ (hop * stride)) for i in range(size)])
 
 
-def call(body, out_shape, name, scratch=(), grant=8):
+def call(body, out_shape, scratch=(), grant=8, far=0):
+    options = {"in_specs": [pl.BlockSpec(memory_space=pltpu.HBM)] * far} if far else {}
     kernel = pl.pallas_call(
         body,
         out_shape=out_shape,
         scratch_shapes=list(scratch),
-        name=name,
         compiler_params=pltpu.CompilerParams(vmem_limit_bytes=grant << 20),
-    )
-    return lambda *values: kernel(*(pltpu.with_memory_space_constraint(v, pltpu.VMEM) for v in values))
+        **options,
+    )
+    space = pltpu.HBM if far else pltpu.VMEM
+    return lambda *values: kernel(*(pltpu.with_memory_space_constraint(v, space) for v in values))
 
 
 def rows_of(value):
@@ -39,7 +42,17 @@
     return jnp.where(place == fill_at, 0.0, turned).reshape(shape)
 
 
-def pack_kernel(feats_ref, ups_ref, out_ref, wide):
+def fetch_kernel(count, *refs):
+    sources, targets, done = refs[:count], refs[count:-1], refs[-1]
+    copies = [pltpu.make_async_copy(*pair, done.at[i]) for i, pair in enumerate(zip(sources, targets))]
+    for copy in copies:
+        copy.start()
+    for copy in copies:
+        copy.wait()
+
+
+def pack_kernel(feats_far, ups_far, out_ref, feats_ref, ups_ref, wide, done):
+    fetch_kernel(2, feats_far, ups_far, feats_ref, ups_ref, done)
     half = out_ref.shape[-1]
     low = feats_ref.shape[1]
     ins = feats_ref.shape[2] // half
@@ -85,14 +98,12 @@
         uc[(1,) + where] = block[:, parts * low :, :].reshape(frames, ho, wo, cout)
         uc[(2,) + where] = jnp.concatenate([before, even], axis=2).astype(BF16)
 
-    by_row = []
-    for b in range(3):
-        sums = None
-        for a in range(3):
-            weight = jnp.concatenate([w1_ref[a * 9 + b * 3 + e] for e in range(3)], axis=1)
-            term = jnp.dot(xs[a * low : (a + total) * low, :], weight, preferred_element_type=F32)
-            sums = term if sums is None else sums + term
-        by_row.append(sums.reshape(total, hi, wi, 3 * cout))
+    stacked = jnp.concatenate([xs[a * low : (a + total) * low, :] for a in range(3)], axis=1)
+    weight = jnp.concatenate(
+        [jnp.concatenate([w1_ref[a * 9 + be] for be in range(9)], axis=1) for a in range(3)], axis=0
+    )
+    sums = jnp.dot(stacked, weight, preferred_element_type=F32).reshape(total, hi, wi, 9 * cout)
+    by_row = [sums[..., b * 3 * cout : (b + 1) * 3 * cout] for b in range(3)]
     zero = jnp.zeros((total, wi, 3 * cout), F32)
     pre_rows = []
     for row in range(hi):
@@ -111,15 +122,19 @@
     ht[...] = rows_of(hidden).T.astype(BF16)
     ft[...] = xs[2 * low :, :].astype(F32).T.astype(BF16)
 
-    back = None
-    for a in range(3):
-        for b in range(3):
-            ups = jnp.concatenate(
-                [rows_of(uc[e, 2 - a : 2 - a + total, 2 - b : 2 - b + ho]) for e in range(3)], axis=1
-            )
-            weight = jnp.concatenate([w2_ref[a * 9 + b * 3 + e] for e in range(3)], axis=1)
-            term = lax.dot_general(ups, weight, (((1,), (1,)), ((), ())), preferred_element_type=F32)
-            back = term if back is None else back + term
+    ups = jnp.concatenate(
+        [rows_of(uc[e, :total, 2 - b : 2 - b + ho]) for b in range(3) for e in range(3)], axis=1
+    )
+    weight = jnp.concatenate(
+        [jnp.concatenate([w2_ref[a * 9 + be] for be in range(9)], axis=1) for a in range(3)], axis=0
+    )
+    parts_of = lax.dot_general(ups, weight, (((1,), (1,)), ((), ())), preferred_element_type=F32)
+    parts_of = parts_of.reshape(total, ho, wo, 3 * cout)
+    back = parts_of[..., 2 * cout :]
+    for a in range(2):
+        lead = 2 - a
+        term = parts_of[lead:, ..., a * cout : (a + 1) * cout]
+        back += jnp.concatenate([term, jnp.zeros((lead,) + term.shape[1:], F32)], axis=0)
     dpre = (back.reshape(slope.shape) * slope).astype(BF16).astype(F32)
     even, odd = dpre[:, :, :wi], dpre[:, :, wi:]
     columns = (odd + move_down(even, wi - 1), even + odd, move_down(odd, 0) + even)
@@ -140,14 +155,19 @@
 
     far_size = dp // 2
     tall, short = cin // dp, cout // dp
-    for j in range(chunk):
-        tap = jnp.minimum(me * chunk + j, 26)
-        a, rest = lax.div(tap, 9), lax.rem(tap, 9)
-        b, e = lax.div(rest, 3), lax.rem(rest, 3)
-        boxes = rows_of(dbox_ref[rest, pl.ds(2 - a, total)])
-        g1[j] = jnp.dot(ft[...], boxes, preferred_element_type=F32)
-        ups = rows_of(uc[e, pl.ds(2 - a, total), pl.ds(2 - b, ho)])
-        g2[j] = jnp.dot(ht[...], ups, preferred_element_type=F32)
+    for j in range(0, chunk, 2):
+        boxes, ups = [], []
+        for k in range(j, min(j + 2, chunk)):
+            tap = jnp.minimum(me * chunk + k, 26)
+            a, rest = lax.div(tap, 9), lax.rem(tap, 9)
+            b, e = lax.div(rest, 3), lax.rem(rest, 3)
+            boxes.append(rows_of(dbox_ref[rest, pl.ds(2 - a, total)]))
+            ups.append(rows_of(uc[e, pl.ds(2 - a, total), pl.ds(2 - b, ho)]))
+        one = jnp.dot(ft[...], jnp.concatenate(boxes, axis=1), preferred_element_type=F32)
+        two = jnp.dot(ht[...], jnp.concatenate(ups, axis=1), preferred_element_type=F32)
+        for k in range(len(boxes)):
+            g1[j + k] = one[:, k * cout : (k + 1) * cout]
+            g2[j + k] = two[:, k * cout : (k + 1) * cout]
     for hop in range(far_size):
         for ref, side in ((keep_ref, core), (send_ref, 1 - core)):
             at = (far ^ hop) * 2 + side
@@ -215,10 +235,22 @@
     packed = call(
         pack_kernel,
         near((frames, low * (cin // cout) + high, cout), BF16),
-        "pack",
-        [pltpu.VMEM((frames * ho, wo, cout), F32)],
+        [
+            pltpu.VMEM((frames, low, cin), BF16),
+            pltpu.VMEM((frames, ho, wo, cout), BF16),
+            pltpu.VMEM((frames * ho, wo, cout), F32),
+            pltpu.SemaphoreType.DMA((2,)),
+        ],
+        far=2,
     )(features.reshape(frames, low, cin), upstream.reshape(frames, ho, wo, cout))
     blocks = [packed] + [swap(packed, "tm", hop) for hop in range(1, tm)]
+
+    w1, w2 = call(
+        lambda *refs: fetch_kernel(2, *refs),
+        (near(w1.shape, BF16), near(w2.shape, BF16)),
+        [pltpu.SemaphoreType.DMA((2,))],
+        far=2,
+    )(w1, w2)
 
     def main_body(*refs):
         main_kernel((tm, dp, hi, wi, chunk), refs[:tm], *refs[tm:])
@@ -230,7 +262,6 @@
             near((far_size, chunk, tall + short, cout), BF16),
             near((9, total + 2, low, cout), BF16),
         ),
-        "main",
         [
             pltpu.VMEM(((total + 2) * low, cin), BF16),
             pltpu.VMEM((3, total + 2, ho + 2, wo, cout), BF16),
@@ -247,23 +278,14 @@
         pair_kernel,
         (near((chunk, tall + short, cout), F32),)
         + tuple(near((chunk, tall + short, cout), BF16) for _ in range(far_size - 1)),
-        "pair",
     )(keep, recv)
     recvs = [swap(value, "dp", hop, 2) for hop, value in enumerate(sends, 1)]
-    feature_grad = call(
-        lambda *refs: input_grad_kernel(frames, *refs),
-        shape((frames * low, cin), BF16),
-        "input_grad",
-    )(dbox, w1)
+    feature_grad = call(lambda *refs: input_grad_kernel(frames, *refs), shape((frames * low, cin), BF16))(dbox, w1)
     factor = 1.0 / math.sqrt(clips * dp * total * high)
-    share = call(
-        lambda *refs: sum_kernel(factor, *refs), near((chunk, tall + short, cout), BF16), "sum"
-    )(own, *recvs)
+    share = call(lambda *refs: sum_kernel(factor, *refs), near((chunk, tall + short, cout), BF16))(own, *recvs)
     shares = [share] + [swap(share, "tm", hop) for hop in range(1, tm)]
     one, two = call(
-        lambda *refs: spread_kernel(tall, *refs),
-        (shape((taps, tall, cout), F32), shape((taps, short, cout), F32)),
-        "spread",
+        lambda *refs: spread_kernel(tall, *refs), (shape((taps, tall, cout), F32), shape((taps, short, cout), F32))
     )(*shares)
     return (
         feature_grad.reshape(features.shape),

time: 39.9 us -> 35.4 us (0.89)
  local copies, waits for them, and re-layouts: 4.23 us -> 0 us
  waiting for transfers between devices: 15.8 us -> 14.1 us
  Pallas kernels: 6.21 us -> 7.75 us
    unnamed x8 -> x0, local copies, waits for them, and re-layouts: 4.23 us -> none
    ppermute x10, waiting for transfers between devices: 15.8 us -> 14.1 us  [swap(): lax.ppermute(value, axis, [(i, i ^ hop * stride) for i in range(size)])]
    pallas_call x6 -> x7, Pallas kernels: 6.21 us -> 7.75 us  [call(): kernel(*(pltpu.with_memory_space_constraint(v, space) for v in values))]
  transfers between devices with their start and end apart: 10 -> 10, of which waited for: 9 -> 9; matrix products, arithmetic and copies ran while one was open for 0% -> 0% of each run, Pallas kernels for 3% -> 9%
where the time goes in v3:
time: 35.4 us; the launch traced here: 35.2 us
  waiting for transfers between devices  14.1 us (40%)
  starting transfers between devices  12.7 us (36%)
  Pallas kernels  7.75 us (22%)
  between operations  0.68 us (2%)
    ppermute x10, waiting for transfers between devices, swap(): lax.ppermute(value, axis, [(i, i ^ hop * stride) for i in range(size)])  14.1 us
    ppermute x10, starting transfers between devices, swap(): lax.ppermute(value, axis, [(i, i ^ hop * stride) for i in range(size)])  12.7 us
    pallas_call x7, Pallas kernels, call(): kernel(*(pltpu.with_memory_space_constraint(v, space) for v in values))  7.75 us
  transfers between devices with their start and end apart: 10, of which 9 were waited for; matrix products, arithmetic and copies ran while one was open for 0% of the time, Pallas kernels for 9%

profile of v3, /device:TPU:0, one launch (start us, length us, event | category | flops | bytes accessed | tf_op | source)
XLA Modules:
  0.0 35.2 jit_solution(10608189400204050522)
XLA Ops:
  0.6 0.9 %shard_map.67.refs_0_ = bf16[4,96,128]{2,1,0:T(8,128)(2,1)S(1)} custom-call(bf16[4,16,256]{2,1,0:T(8,128)(2,1)} %bitcast.11, bf16[4,4,16,128]{3,2,1,0:T(8,128)(2,1)} %bitcast.9), custom_call_target="tpu_custom_call" | custom-call | tf_op jit(solution)/shard_map/pallas_call | solution.py:29
  1.5 4.0 %collective-permute-start.2 = (bf16[4,96,128]{2,1,0:T(8,128)(2,1)S(1)}, bf16[4,96,128]{2,1,0:T(8,128)(2,1)S(1)}, u32[]{:S(2)}, u32[]{:S(2)}) collective-permute-start(bf16[4,96,128]{2,1,0:T(8,128)(2,1)S(1)} %shard_map.67.refs_0_), channel_id=1, source_target_pairs={{0,24},{8,16},{16,8},{24,0},{1,25},{9,17},{17,9},{25,1},{2,26},{10... | collective-permute-start | bytes 294920 | tf_op jit(solution)/shard_map/ppermute | solution.py:16
  5.5 0.5 %collective-permute-start.1 = (bf16[4,96,128]{2,1,0:T(8,128)(2,1)S(1)}, bf16[4,96,128]{2,1,0:T(8,128)(2,1)S(1)}, u32[]{:S(2)}, u32[]{:S(2)}) collective-permute-start(bf16[4,96,128]{2,1,0:T(8,128)(2,1)S(1)} %shard_map.67.refs_0_), channel_id=1, source_target_pairs={{0,16},{8,24},{16,0},{24,8},{1,17},{9,25},{17,1},{25,9},{2,18},{10... | collective-permute-start | bytes 294920 | tf_op jit(solution)/shard_map/ppermute | solution.py:16
  6.0 0.1 collective-permute-start
  6.2 1.7 %shard_map.68 = (bf16[27,256,128]{2,1,0:T(8,128)(2,1)S(1)}, bf16[27,128,128]{2,1,0:T(8,128)(2,1)S(1)}) custom-call(bf16[27,256,128]{2,1,0:T(8,128)(2,1)} %bitcast.7, bf16[27,128,128]{2,1,0:T(8,128)(2,1)} %bitcast.8), custom_call_target="tpu_custom_call" | custom-call | tf_op jit(solution)/shard_map/pallas_call | solution.py:29
  7.9 0.8 %collective-permute-done.2.refs_3_ = bf16[4,96,128]{2,1,0:T(8,128)(2,1)S(1)} collective-permute-done((bf16[4,96,128]{2,1,0:T(8,128)(2,1)S(1)}, bf16[4,96,128]{2,1,0:T(8,128)(2,1)S(1)}, u32[]{:S(2)}, u32[]{:S(2)}) %collective-permute-start.2) | collective-permute-done | bytes 98336 | tf_op jit(solution)/shard_map/ppermute | solution.py:16
  8.7 1.7 %collective-permute-done.1.refs_2_ = bf16[4,96,128]{2,1,0:T(8,128)(2,1)S(1)} collective-permute-done((bf16[4,96,128]{2,1,0:T(8,128)(2,1)S(1)}, bf16[4,96,128]{2,1,0:T(8,128)(2,1)S(1)}, u32[]{:S(2)}, u32[]{:S(2)}) %collective-permute-start.1) | collective-permute-done | bytes 98336 | tf_op jit(solution)/shard_map/ppermute | solution.py:16
  10.4 0.3 collective-permute-done.refs_1_
  10.8 2.8 %shard_map.69 = (f32[4,7,48,128]{3,2,1,0:T(8,128)S(1)}, bf16[4,7,48,128]{3,2,1,0:T(8,128)(2,1)S(1)}, bf16[9,18,16,128]{3,2,1,0:T(8,128)(2,1)S(1)}) custom-call(bf16[4,96,128]{2,1,0:T(8,128)(2,1)S(1)} %shard_map.67.refs_0_, bf16[4,96,128]{2,1,0:T(8,128)(2,1)S(1)} %collective-permute-done.refs_1_, bf16[4,96,128]{2,1,0:T(8,128)(2,1)S(1)} %collective-permute-done.1.refs_2_, ...), custom_call_target="tpu_custom_call" | custom-call | tf_op jit(solution)/shard_map/pallas_call | solution.py:29
  13.5 0.1 collective-permute-start.3
  13.6 1.6 %collective-permute-done.3.recv_ref = bf16[4,7,48,128]{3,2,1,0:T(8,128)(2,1)S(1)} collective-permute-done((bf16[4,7,48,128]{3,2,1,0:T(8,128)(2,1)S(1)}, bf16[4,7,48,128]{3,2,1,0:T(8,128)(2,1)S(1)}, u32[]{:S(2)}, u32[]{:S(2)}) %collective-permute-start.3) | collective-permute-done | bytes 344096 | tf_op jit(solution)/shard_map/ppermute | solution.py:16
  15.3 0.1 shard_map.71
  15.3 1.6 %collective-permute-start.4 = (bf16[7,48,128]{2,1,0:T(8,128)(2,1)S(1)}, bf16[7,48,128]{2,1,0:T(8,128)(2,1)S(1)}, u32[]{:S(2)}, u32[]{:S(2)}) collective-permute-start(bf16[7,48,128]{2,1,0:T(8,128)(2,1)S(1)} %get-tuple-element.20), channel_id=1, source_target_pairs={{0,2},{1,3},{2,0},{3,1},{4,6},{5,7},{6,4},{7,5},{8,10},{9,11},{10,... | collective-permute-start | bytes 258056 | tf_op jit(solution)/shard_map/ppermute | solution.py:16
  17.0 2.6 %collective-permute-start.5 = (bf16[7,48,128]{2,1,0:T(8,128)(2,1)S(1)}, bf16[7,48,128]{2,1,0:T(8,128)(2,1)S(1)}, u32[]{:S(2)}, u32[]{:S(2)}) collective-permute-start(bf16[7,48,128]{2,1,0:T(8,128)(2,1)S(1)} %get-tuple-element.21), channel_id=1, source_target_pairs={{0,4},{1,5},{2,6},{3,7},{4,0},{5,1},{6,2},{7,3},{8,12},{9,13},{10,... | collective-permute-start | bytes 258056 | tf_op jit(solution)/shard_map/ppermute | solution.py:16
  19.5 0.2 collective-permute-start.6
  19.8 0.2 collective-permute-done.4.refs_1_
  20.0 6.8 %collective-permute-done.5.refs_2_ = bf16[7,48,128]{2,1,0:T(8,128)(2,1)S(1)} collective-permute-done((bf16[7,48,128]{2,1,0:T(8,128)(2,1)S(1)}, bf16[7,48,128]{2,1,0:T(8,128)(2,1)S(1)}, u32[]{:S(2)}, u32[]{:S(2)}) %collective-permute-start.5) | collective-permute-done | bytes 86048 | tf_op jit(solution)/shard_map/ppermute | solution.py:16
  26.7 0.0 collective-permute-done.6.refs_3_
  26.7 0.1 shard_map.72.refs_0_
  26.8 1.7 %collective-permute-start.9 = (bf16[7,48,128]{2,1,0:T(8,128)(2,1)S(1)}, bf16[7,48,128]{2,1,0:T(8,128)(2,1)S(1)}, u32[]{:S(2)}, u32[]{:S(2)}) collective-permute-start(bf16[7,48,128]{2,1,0:T(8,128)(2,1)S(1)} %shard_map.72.refs_0_), channel_id=1, source_target_pairs={{0,24},{8,16},{16,8},{24,0},{1,25},{9,17},{17,9},{25,1},{2,26},{10... | collective-permute-start | bytes 258056 | tf_op jit(solution)/shard_map/ppermute | solution.py:16
  28.5 1.3 %collective-permute-start.8 = (bf16[7,48,128]{2,1,0:T(8,128)(2,1)S(1)}, bf16[7,48,128]{2,1,0:T(8,128)(2,1)S(1)}, u32[]{:S(2)}, u32[]{:S(2)}) collective-permute-start(bf16[7,48,128]{2,1,0:T(8,128)(2,1)S(1)} %shard_map.72.refs_0_), channel_id=1, source_target_pairs={{0,16},{8,24},{16,0},{24,8},{1,17},{9,25},{17,1},{25,9},{2,18},{10... | collective-permute-start | bytes 258056 | tf_op jit(solution)/shard_map/ppermute | solution.py:16
  29.8 0.6 %collective-permute-start.7 = (bf16[7,48,128]{2,1,0:T(8,128)(2,1)S(1)}, bf16[7,48,128]{2,1,0:T(8,128)(2,1)S(1)}, u32[]{:S(2)}, u32[]{:S(2)}) collective-permute-start(bf16[7,48,128]{2,1,0:T(8,128)(2,1)S(1)} %shard_map.72.refs_0_), channel_id=1, source_target_pairs={{0,8},{8,0},{16,24},{24,16},{1,9},{9,1},{17,25},{25,17},{2,10},{10... | collective-permute-start | bytes 258056 | tf_op jit(solution)/shard_map/ppermute | solution.py:16
  30.3 1.3 %shard_map.70 = bf16[64,256]{1,0:T(8,128)(2,1)} custom-call(bf16[9,18,16,128]{3,2,1,0:T(8,128)(2,1)S(1)} %get-tuple-element.16.refs_0_, bf16[27,256,128]{2,1,0:T(8,128)(2,1)S(1)} %get-tuple-element.14.refs_4_.refs_1_), custom_call_target="tpu_custom_call" | custom-call | tf_op jit(solution)/shard_map/pallas_call | solution.py:29
  31.6 0.6 %collective-permute-done.9.refs_3_ = bf16[7,48,128]{2,1,0:T(8,128)(2,1)S(1)} collective-permute-done((bf16[7,48,128]{2,1,0:T(8,128)(2,1)S(1)}, bf16[7,48,128]{2,1,0:T(8,128)(2,1)S(1)}, u32[]{:S(2)}, u32[]{:S(2)}) %collective-permute-start.9) | collective-permute-done | bytes 86048 | tf_op jit(solution)/shard_map/ppermute | solution.py:16
  32.2 0.9 %collective-permute-done.8.refs_2_ = bf16[7,48,128]{2,1,0:T(8,128)(2,1)S(1)} collective-permute-done((bf16[7,48,128]{2,1,0:T(8,128)(2,1)S(1)}, bf16[7,48,128]{2,1,0:T(8,128)(2,1)S(1)}, u32[]{:S(2)}, u32[]{:S(2)}) %collective-permute-start.8) | collective-permute-done | bytes 86048 | tf_op jit(solution)/shard_map/ppermute | solution.py:16
  33.2 1.1 %collective-permute-done.7.refs_1_ = bf16[7,48,128]{2,1,0:T(8,128)(2,1)S(1)} collective-permute-done((bf16[7,48,128]{2,1,0:T(8,128)(2,1)S(1)}, bf16[7,48,128]{2,1,0:T(8,128)(2,1)S(1)}, u32[]{:S(2)}, u32[]{:S(2)}) %collective-permute-start.7) | collective-permute-done | bytes 86048 | tf_op jit(solution)/shard_map/ppermute | solution.py:16
  34.3 1.0 %shard_map.73 = (f32[27,32,128]{2,1,0:T(8,128)}, f32[27,16,128]{2,1,0:T(8,128)}) custom-call(bf16[7,48,128]{2,1,0:T(8,128)(2,1)S(1)} %shard_map.72.refs_0_, bf16[7,48,128]{2,1,0:T(8,128)(2,1)S(1)} %collective-permute-done.7.refs_1_, bf16[7,48,128]{2,1,0:T(8,128)(2,1)S(1)} %collective-permute-done.8.refs_2_, ...), custom_call_target="tpu_custom_call" | custom-call | tf_op jit(solution)/shard_map/pallas_call | solution.py:29
Async XLA Ops:
  1.5 7.2 %collective-permute-start.2 = (bf16[4,96,128]{2,1,0:T(8,128)(2,1)S(1)}, bf16[4,96,128]{2,1,0:T(8,128)(2,1)S(1)}, u32[]{:S(2)}, u32[]{:S(2)}) collective-permute-start(bf16[4,96,128]{2,1,0:T(8,128)(2,1)S(1)} %shard_map.67.refs_0_), channel_id=1, source_target_pairs={{0,24},{8,16},{16,8},{24,0},{1,25},{9,17},{17,9},{25,1},{2,26},{10... | collective-permute-start | bytes 294920 | tf_op jit(solution)/shard_map/ppermute | solution.py:16
  5.5 4.9 %collective-permute-start.1 = (bf16[4,96,128]{2,1,0:T(8,128)(2,1)S(1)}, bf16[4,96,128]{2,1,0:T(8,128)(2,1)S(1)}, u32[]{:S(2)}, u32[]{:S(2)}) collective-permute-start(bf16[4,96,128]{2,1,0:T(8,128)(2,1)S(1)} %shard_map.67.refs_0_), channel_id=1, source_target_pairs={{0,16},{8,24},{16,0},{24,8},{1,17},{9,25},{17,1},{25,9},{2,18},{10... | collective-permute-start | bytes 294920 | tf_op jit(solution)/shard_map/ppermute | solution.py:16
  6.0 4.7 %collective-permute-start = (bf16[4,96,128]{2,1,0:T(8,128)(2,1)S(1)}, bf16[4,96,128]{2,1,0:T(8,128)(2,1)S(1)}, u32[]{:S(2)}, u32[]{:S(2)}) collective-permute-start(bf16[4,96,128]{2,1,0:T(8,128)(2,1)S(1)} %shard_map.67.refs_0_), channel_id=1, source_target_pairs={{0,8},{8,0},{16,24},{24,16},{1,9},{9,1},{17,25},{25,17},{2,10},{10... | collective-permute-start | bytes 294920 | tf_op jit(solution)/shard_map/ppermute | solution.py:16
  13.5 1.7 %collective-permute-start.3 = (bf16[4,7,48,128]{3,2,1,0:T(8,128)(2,1)S(1)}, bf16[4,7,48,128]{3,2,1,0:T(8,128)(2,1)S(1)}, u32[]{:S(2)}, u32[]{:S(2)}) collective-permute-start(bf16[4,7,48,128]{3,2,1,0:T(8,128)(2,1)S(1)} %get-tuple-element.18), channel_id=1, source_target_pairs={{0,1},{1,0},{2,3},{3,2},{4,5},{5,4},{6,7},{7,6},{8,9},{9,8},{10,11... | collective-permute-start | bytes 1032200 | tf_op jit(solution)/shard_map/ppermute | solution.py:16
  15.3 4.6 %collective-permute-start.4 = (bf16[7,48,128]{2,1,0:T(8,128)(2,1)S(1)}, bf16[7,48,128]{2,1,0:T(8,128)(2,1)S(1)}, u32[]{:S(2)}, u32[]{:S(2)}) collective-permute-start(bf16[7,48,128]{2,1,0:T(8,128)(2,1)S(1)} %get-tuple-element.20), channel_id=1, source_target_pairs={{0,2},{1,3},{2,0},{3,1},{4,6},{5,7},{6,4},{7,5},{8,10},{9,11},{10,... | collective-permute-start | bytes 258056 | tf_op jit(solution)/shard_map/ppermute | solution.py:16
  17.0 9.8 %collective-permute-start.5 = (bf16[7,48,128]{2,1,0:T(8,128)(2,1)S(1)}, bf16[7,48,128]{2,1,0:T(8,128)(2,1)S(1)}, u32[]{:S(2)}, u32[]{:S(2)}) collective-permute-start(bf16[7,48,128]{2,1,0:T(8,128)(2,1)S(1)} %get-tuple-element.21), channel_id=1, source_target_pairs={{0,4},{1,5},{2,6},{3,7},{4,0},{5,1},{6,2},{7,3},{8,12},{9,13},{10,... | collective-permute-start | bytes 258056 | tf_op jit(solution)/shard_map/ppermute | solution.py:16
  19.5 7.2 %collective-permute-start.6 = (bf16[7,48,128]{2,1,0:T(8,128)(2,1)S(1)}, bf16[7,48,128]{2,1,0:T(8,128)(2,1)S(1)}, u32[]{:S(2)}, u32[]{:S(2)}) collective-permute-start(bf16[7,48,128]{2,1,0:T(8,128)(2,1)S(1)} %get-tuple-element.22), channel_id=1, source_target_pairs={{0,6},{1,7},{2,4},{3,5},{4,2},{5,3},{6,0},{7,1},{8,14},{9,15},{10,... | collective-permute-start | bytes 258056 | tf_op jit(solution)/shard_map/ppermute | solution.py:16
  26.8 5.5 %collective-permute-start.9 = (bf16[7,48,128]{2,1,0:T(8,128)(2,1)S(1)}, bf16[7,48,128]{2,1,0:T(8,128)(2,1)S(1)}, u32[]{:S(2)}, u32[]{:S(2)}) collective-permute-start(bf16[7,48,128]{2,1,0:T(8,128)(2,1)S(1)} %shard_map.72.refs_0_), channel_id=1, source_target_pairs={{0,24},{8,16},{16,8},{24,0},{1,25},{9,17},{17,9},{25,1},{2,26},{10... | collective-permute-start | bytes 258056 | tf_op jit(solution)/shard_map/ppermute | solution.py:16
  28.5 4.7 %collective-permute-start.8 = (bf16[7,48,128]{2,1,0:T(8,128)(2,1)S(1)}, bf16[7,48,128]{2,1,0:T(8,128)(2,1)S(1)}, u32[]{:S(2)}, u32[]{:S(2)}) collective-permute-start(bf16[7,48,128]{2,1,0:T(8,128)(2,1)S(1)} %shard_map.72.refs_0_), channel_id=1, source_target_pairs={{0,16},{8,24},{16,0},{24,8},{1,17},{9,25},{17,1},{25,9},{2,18},{10... | collective-permute-start | bytes 258056 | tf_op jit(solution)/shard_map/ppermute | solution.py:16
  29.8 4.5 %collective-permute-start.7 = (bf16[7,48,128]{2,1,0:T(8,128)(2,1)S(1)}, bf16[7,48,128]{2,1,0:T(8,128)(2,1)S(1)}, u32[]{:S(2)}, u32[]{:S(2)}) collective-permute-start(bf16[7,48,128]{2,1,0:T(8,128)(2,1)S(1)} %shard_map.72.refs_0_), channel_id=1, source_target_pairs={{0,8},{8,0},{16,24},{24,16},{1,9},{9,1},{17,25},{25,17},{2,10},{10... | collective-permute-start | bytes 258056 | tf_op jit(solution)/shard_map/ppermute | solution.py:16

commit v4 on v3

--- a/solution.py
+++ b/solution.py
@@ -66,8 +66,91 @@
     out_ref[:, ins * low :, :] = both.reshape(frames, ho * wo, half).astype(BF16)
 
 
-def main_kernel(dims, blocks, w1_ref, w2_ref, keep_ref, send_ref, dbox_ref, xs, uc, ht, ft, g1, g2):
-    tm, dp, hi, wi, chunk = dims
+def shifted(block, skip, ho, wi):
+    frames, _, cout = block.shape
+    ups = block[:, skip:, :]
+    wide = ups.reshape(frames, ho, 2, wi, cout).astype(F32)
+    even, odd = wide[:, :, 0], wide[:, :, 1]
+    after = move_down(even, wi - 1)
+    before = move_down(odd, 0)
+    return (
+        jnp.concatenate([odd, after], axis=2).astype(BF16),
+        ups.reshape(frames, ho, 2 * wi, cout),
+        jnp.concatenate([before, even], axis=2).astype(BF16),
+    )
+
+
+def clear_edges(uc):
+    rows = uc.shape[2]
+    for row in (0, rows - 1):
+        uc[:, :, row] = jnp.zeros(uc.shape[:2] + uc.shape[3:], BF16)
+
+
+def through_second(uc, starts, frames, w2_ref):
+    ho = uc.shape[2] - 2
+    ups = jnp.concatenate(
+        [
+            jnp.concatenate([rows_of(uc[e, pl.ds(start, frames), 2 - b : 2 - b + ho]) for start in starts], axis=0)
+            for b in range(3)
+            for e in range(3)
+        ],
+        axis=1,
+    )
+    weight = jnp.concatenate(
+        [jnp.concatenate([w2_ref[a * 9 + be] for be in range(9)], axis=1) for a in range(3)], axis=0
+    )
+    return lax.dot_general(ups, weight, (((1,), (1,)), ((), ())), preferred_element_type=F32)
+
+
+def early_kernel(dims, one, two, w2_ref, out_ref, uc):
+    hi, wi, skip = dims
+    frames = one.shape[0]
+    clear_edges(uc)
+    for at, block in enumerate((one, two)):
+        for e, value in enumerate(shifted(block, skip, 2 * hi, wi)):
+            uc[e, at * frames : (at + 1) * frames, 1 : 2 * hi + 1] = value
+    out_ref[...] = through_second(uc, [0], 2 * frames, w2_ref)
+
+
+def kernel_grads(dims, same_core, ft, ht, uc, dbox_ref, out_ref):
+    _, dp, hi, _, chunk = dims
+    me, mine = lax.axis_index("tm"), lax.axis_index("dp")
+    core, far = lax.rem(mine, 2), lax.div(mine, 2)
+    side = core if same_core else 1 - core
+    total, ho = dbox_ref.shape[1] - 2, 2 * hi
+    cout = dbox_ref.shape[-1]
+    tall, short = ft.shape[1], ht.shape[1]
+    hops = range(dp // 2)
+
+    def picked(ref):
+        return jnp.concatenate([ref[(far ^ hop) * 2 + side] for hop in hops], axis=0).astype(BF16)
+
+    wide, narrow = picked(ft), picked(ht)
+    taps = []
+    for j in range(chunk):
+        tap = jnp.minimum(me * chunk + j, 26)
+        rest = lax.rem(tap, 9)
+        taps.append((lax.div(tap, 9), lax.div(rest, 3), lax.rem(rest, 3)))
+    for j in range(0, chunk, 2):
+        wanted = taps[j : j + 2]
+        ups = [rows_of(uc[e, pl.ds(2 - a, total), pl.ds(2 - b, ho)]) for a, b, e in wanted]
+        two = jnp.dot(narrow, jnp.concatenate(ups, axis=1), preferred_element_type=F32)
+        for hop in hops:
+            for k in range(len(wanted)):
+                part = two[hop * short : (hop + 1) * short, k * cout : (k + 1) * cout]
+                out_ref[hop, j + k, tall:] = part.astype(out_ref.dtype)
+    for j in range(0, chunk, 2):
+        wanted = taps[j : j + 2]
+        boxes = [rows_of(dbox_ref[b * 3 + e, pl.ds(2 - a, total)]) for a, b, e in wanted]
+        one = jnp.dot(wide, jnp.concatenate(boxes, axis=1), preferred_element_type=F32)
+        for hop in hops:
+            for k in range(len(wanted)):
+                part = one[hop * tall : (hop + 1) * tall, k * cout : (k + 1) * cout]
+                out_ref[hop, j + k, :tall] = part.astype(out_ref.dtype)
+
+
+def main_kernel(dims, blocks, w1_ref, w2_ref, early_ref, send_ref, ft, ht, uc, dbox_ref, xs, zs):
+    tm, _, hi, wi, _ = dims
     ho, wo = 2 * hi, 2 * wi
     low = hi * wi
     frames = blocks[0].shape[0]
@@ -75,28 +158,18 @@
     cin, cout = w1_ref.shape[1], w1_ref.shape[2]
     parts = cin // cout
     me = lax.axis_index("tm")
-    mine = lax.axis_index("dp")
-    core, far = lax.rem(mine, 2), lax.div(mine, 2)
 
     xs[: 2 * low] = jnp.zeros((2 * low, cin), BF16)
     uc[:, total:] = jnp.zeros((3, 2) + uc.shape[2:], BF16)
-    uc[:, :, 0] = jnp.zeros((3, total + 2) + uc.shape[3:], BF16)
-    uc[:, :, ho + 1] = jnp.zeros((3, total + 2) + uc.shape[3:], BF16)
-    for hop, block in enumerate(blocks):
-        start = (me ^ hop) * frames
+    clear_edges(uc)
+    starts = [(me ^ hop) * frames for hop in range(tm)]
+    for start, block in zip(starts, blocks):
         feats = jnp.concatenate(
             [rows_of(block[:, part * low : (part + 1) * low, :]) for part in range(parts)], axis=1
         )
         xs[pl.ds(pl.multiple_of((start + 2) * low, low), frames * low), :] = feats
-        ups = block[:, parts * low :, :].reshape(frames, ho, 2, wi, cout)
-        wide = ups.astype(F32)
-        even, odd = wide[:, :, 0], wide[:, :, 1]
-        after = move_down(even, wi - 1)
-        before = move_down(odd, 0)
-        where = (pl.ds(start, frames), slice(1, ho + 1))
-        uc[(0,) + where] = jnp.concatenate([odd, after], axis=2).astype(BF16)
-        uc[(1,) + where] = block[:, parts * low :, :].reshape(frames, ho, wo, cout)
-        uc[(2,) + where] = jnp.concatenate([before, even], axis=2).astype(BF16)
+        for e, value in enumerate(shifted(block, parts * low, ho, wi)):
+            uc[e, pl.ds(start, frames), 1 : ho + 1] = value
 
     stacked = jnp.concatenate([xs[a * low : (a + total) * low, :] for a in range(3)], axis=1)
     weight = jnp.concatenate(
@@ -119,17 +192,15 @@
     sigma = 1.0 / (1.0 + jnp.exp(-pre))
     hidden = pre * sigma
     slope = sigma * (1.0 + pre * (1.0 - sigma))
-    ht[...] = rows_of(hidden).T.astype(BF16)
-    ft[...] = xs[2 * low :, :].astype(F32).T.astype(BF16)
-
-    ups = jnp.concatenate(
-        [rows_of(uc[e, :total, 2 - b : 2 - b + ho]) for b in range(3) for e in range(3)], axis=1
-    )
-    weight = jnp.concatenate(
-        [jnp.concatenate([w2_ref[a * 9 + be] for be in range(9)], axis=1) for a in range(3)], axis=0
-    )
-    parts_of = lax.dot_general(ups, weight, (((1,), (1,)), ((), ())), preferred_element_type=F32)
-    parts_of = parts_of.reshape(total, ho, wo, 3 * cout)
+    ht[...] = rows_of(hidden).T.reshape(ht.shape)
+    ft[...] = xs[2 * low :, :].astype(F32).T.reshape(ft.shape)
+
+    late = starts[1:-1]
+    for found, places in ((through_second(uc, late, frames, w2_ref), late), (early_ref[...], starts[:: tm - 1])):
+        found = found.reshape(len(places), frames, ho, wo, 3 * cout)
+        for at, start in enumerate(places):
+            zs[pl.ds(start, frames)] = found[at]
+    parts_of = zs[...]
     back = parts_of[..., 2 * cout :]
     for a in range(2):
         lead = 2 - a
@@ -153,26 +224,7 @@
             dbox_ref[b * 3 + e, :total] = box.astype(BF16)
     dbox_ref[:, total:] = jnp.zeros((9, 2, low, cout), BF16)
 
-    far_size = dp // 2
-    tall, short = cin // dp, cout // dp
-    for j in range(0, chunk, 2):
-        boxes, ups = [], []
-        for k in range(j, min(j + 2, chunk)):
-            tap = jnp.minimum(me * chunk + k, 26)
-            a, rest = lax.div(tap, 9), lax.rem(tap, 9)
-            b, e = lax.div(rest, 3), lax.rem(rest, 3)
-            boxes.append(rows_of(dbox_ref[rest, pl.ds(2 - a, total)]))
-            ups.append(rows_of(uc[e, pl.ds(2 - a, total), pl.ds(2 - b, ho)]))
-        one = jnp.dot(ft[...], jnp.concatenate(boxes, axis=1), preferred_element_type=F32)
-        two = jnp.dot(ht[...], jnp.concatenate(ups, axis=1), preferred_element_type=F32)
-        for k in range(len(boxes)):
-            g1[j + k] = one[:, k * cout : (k + 1) * cout]
-            g2[j + k] = two[:, k * cout : (k + 1) * cout]
-    for hop in range(far_size):
-        for ref, side in ((keep_ref, core), (send_ref, 1 - core)):
-            at = (far ^ hop) * 2 + side
-            ref[hop, :, :tall] = g1[:, pl.ds(pl.multiple_of(at * tall, tall), tall)].astype(ref.dtype)
-            ref[hop, :, tall:] = g2[:, pl.ds(pl.multiple_of(at * short, short), short)].astype(ref.dtype)
+    kernel_grads(dims, False, ft, ht, uc, dbox_ref, send_ref)
 
 
 def input_grad_kernel(frames, dbox_ref, w1_ref, out_ref):
@@ -252,27 +304,36 @@
         far=2,
     )(w1, w2)
 
+    early = call(
+        lambda *refs: early_kernel((hi, wi, low * (cin // cout)), *refs),
+        near((2 * frames * high, 3 * cout), F32),
+        [pltpu.VMEM((3, 2 * frames, ho + 2, wo, cout), BF16)],
+    )(blocks[0], blocks[-1], w2)
+
     def main_body(*refs):
         main_kernel((tm, dp, hi, wi, chunk), refs[:tm], *refs[tm:])
 
-    keep, send, dbox = call(
+    send, *held = call(
         main_body,
         (
-            near((far_size, chunk, tall + short, cout), F32),
             near((far_size, chunk, tall + short, cout), BF16),
+            near((dp, tall, total * low), F32),
+            near((dp, short, total * high), F32),
+            near((3, total + 2, ho + 2, wo, cout), BF16),
             near((9, total + 2, low, cout), BF16),
         ),
         [
             pltpu.VMEM(((total + 2) * low, cin), BF16),
-            pltpu.VMEM((3, total + 2, ho + 2, wo, cout), BF16),
-            pltpu.VMEM((cout, total * high), BF16),
-            pltpu.VMEM((cin, total * low), BF16),
-            pltpu.VMEM((chunk, cin, cout), F32),
-            pltpu.VMEM((chunk, cout, cout), F32),
+            pltpu.VMEM((total, ho, wo, 3 * cout), F32),
         ],
         grant=32,
-    )(*blocks, w1, w2)
-
+    )(*blocks, w1, w2, early)
+    dbox = held[-1]
+
+    keep = call(
+        lambda *refs: kernel_grads((tm, dp, hi, wi, chunk), True, *refs),
+        near((far_size, chunk, tall + short, cout), F32),
+    )(*held)
     recv = swap(send, "dp", 1)
     own, *sends = call(
         pair_kernel,

time: 35.4 us -> 34.8 us (0.983)
  waiting for transfers between devices: 14.1 us -> 12.7 us
  Pallas kernels: 7.75 us -> 8.57 us
    ppermute x10, waiting for transfers between devices: 14.1 us -> 12.7 us  [swap(): lax.ppermute(value, axis, [(i, i ^ hop * stride) for i in range(size)])]
    pallas_call x7 -> x9, Pallas kernels: 7.75 us -> 8.57 us  [call(): kernel(*(pltpu.with_memory_space_constraint(v, space) for v in values))]
  transfers between devices with their start and end apart: 10 -> 10, of which waited for: 9 -> 9; matrix products, arithmetic and copies ran while one was open for 0% -> 0% of each run, Pallas kernels for 9% -> 13%
where the time goes in v4:
time: 34.8 us; the launch traced here: 34.6 us
  starting transfers between devices  12.7 us (36%)
  waiting for transfers between devices  12.7 us (36%)
  Pallas kernels  8.57 us (25%)
  between operations  0.69 us (2%)
    ppermute x10, starting transfers between devices, swap(): lax.ppermute(value, axis, [(i, i ^ hop * stride) for i in range(size)])  12.7 us
    ppermute x10, waiting for transfers between devices, swap(): lax.ppermute(value, axis, [(i, i ^ hop * stride) for i in range(size)])  12.7 us
    pallas_call x9, Pallas kernels, call(): kernel(*(pltpu.with_memory_space_constraint(v, space) for v in values))  8.57 us
  transfers between devices with their start and end apart: 10, of which 9 were waited for; matrix products, arithmetic and copies ran while one was open for 0% of the time, Pallas kernels for 13%

profile of v4, /device:TPU:0, one launch (start us, length us, event | category | flops | bytes accessed | tf_op | source)
XLA Modules:
  0.0 34.6 jit_solution(17403955345836648391)
XLA Ops:
  0.6 0.9 %shard_map.67.refs_0_ = bf16[4,96,128]{2,1,0:T(8,128)(2,1)S(1)} custom-call(bf16[4,16,256]{2,1,0:T(8,128)(2,1)} %bitcast.11, bf16[4,4,16,128]{3,2,1,0:T(8,128)(2,1)} %bitcast.9), custom_call_target="tpu_custom_call" | custom-call | tf_op jit(solution)/shard_map/pallas_call | solution.py:29
  1.5 4.0 %collective-permute-start.2 = (bf16[4,96,128]{2,1,0:T(8,128)(2,1)S(1)}, bf16[4,96,128]{2,1,0:T(8,128)(2,1)S(1)}, u32[]{:S(2)}, u32[]{:S(2)}) collective-permute-start(bf16[4,96,128]{2,1,0:T(8,128)(2,1)S(1)} %shard_map.67.refs_0_), channel_id=1, source_target_pairs={{0,24},{8,16},{16,8},{24,0},{1,25},{9,17},{17,9},{25,1},{2,26},{10... | collective-permute-start | bytes 294920 | tf_op jit(solution)/shard_map/ppermute | solution.py:16
  5.5 0.5 %collective-permute-start.1 = (bf16[4,96,128]{2,1,0:T(8,128)(2,1)S(1)}, bf16[4,96,128]{2,1,0:T(8,128)(2,1)S(1)}, u32[]{:S(2)}, u32[]{:S(2)}) collective-permute-start(bf16[4,96,128]{2,1,0:T(8,128)(2,1)S(1)} %shard_map.67.refs_0_), channel_id=1, source_target_pairs={{0,16},{8,24},{16,0},{24,8},{1,17},{9,25},{17,1},{25,9},{2,18},{10... | collective-permute-start | bytes 294920 | tf_op jit(solution)/shard_map/ppermute | solution.py:16
  6.0 0.1 collective-permute-start
  6.2 1.7 %shard_map.68 = (bf16[27,256,128]{2,1,0:T(8,128)(2,1)S(1)}, bf16[27,128,128]{2,1,0:T(8,128)(2,1)S(1)}) custom-call(bf16[27,256,128]{2,1,0:T(8,128)(2,1)} %bitcast.7, bf16[27,128,128]{2,1,0:T(8,128)(2,1)} %bitcast.8), custom_call_target="tpu_custom_call" | custom-call | tf_op jit(solution)/shard_map/pallas_call | solution.py:29
  7.9 0.8 %collective-permute-done.2.refs_1_.refs_3_ = bf16[4,96,128]{2,1,0:T(8,128)(2,1)S(1)} collective-permute-done((bf16[4,96,128]{2,1,0:T(8,128)(2,1)S(1)}, bf16[4,96,128]{2,1,0:T(8,128)(2,1)S(1)}, u32[]{:S(2)}, u32[]{:S(2)}) %collective-permute-start.2) | collective-permute-done | bytes 98336 | tf_op jit(solution)/shard_map/ppermute | solution.py:16
  8.7 0.8 %shard_map.69.refs_6_ = f32[512,384]{1,0:T(8,128)S(1)} custom-call(bf16[4,96,128]{2,1,0:T(8,128)(2,1)S(1)} %shard_map.67.refs_0_, bf16[4,96,128]{2,1,0:T(8,128)(2,1)S(1)} %collective-permute-done.2.refs_1_.refs_3_, bf16[27,128,128]{2,1,0:T(8,128)(2,1)S(1)} %get-tuple-element.17.refs_2_.refs_5_), custom_call_target="tpu_custom_call" | custom-call | tf_op jit(solution)/shard_map/pallas_call | solution.py:29
  9.6 0.9 %collective-permute-done.1.refs_2_ = bf16[4,96,128]{2,1,0:T(8,128)(2,1)S(1)} collective-permute-done((bf16[4,96,128]{2,1,0:T(8,128)(2,1)S(1)}, bf16[4,96,128]{2,1,0:T(8,128)(2,1)S(1)}, u32[]{:S(2)}, u32[]{:S(2)}) %collective-permute-start.1) | collective-permute-done | bytes 98336 | tf_op jit(solution)/shard_map/ppermute | solution.py:16
  10.4 0.3 collective-permute-done.refs_1_
  10.8 2.2 %shard_map.70 = (bf16[4,7,48,128]{3,2,1,0:T(8,128)(2,1)S(1)}, f32[8,32,256]{2,1,0:T(8,128)S(1)}, f32[8,16,1024]{2,1,0:T(8,128)S(1)}, bf16[3,18,6,16,128]{4,3,2,1...) custom-call(bf16[4,96,128]{2,1,0:T(8,128)(2,1)S(1)} %shard_map.67.refs_0_, ...), custom_call_target="tpu_custom_call" | custom-call | tf_op jit(solution)/shard_map/pallas_call | solution.py:29
  12.9 0.1 collective-permute-start.3
  13.0 0.6 %shard_map.72.keep_ref = f32[4,7,48,128]{3,2,1,0:T(8,128)S(1)} custom-call(f32[8,32,256]{2,1,0:T(8,128)S(1)} %get-tuple-element.19.refs_0_, f32[8,16,1024]{2,1,0:T(8,128)S(1)} %get-tuple-element.20.refs_1_, bf16[3,18,6,16,128]{4,3,2,1,0:T(8,128)(2,1)S(1)} %get-tuple-element.21.refs_2_, bf16[9,18,16,128]{3,2,1,0:T(8,128)(2,1)S(1)} %get-tuple-element.18.refs_0_.refs_3_), custom_call_target="tpu_custom_call" | custom-call | tf_op jit(solution)/shard_map/pallas_call | solution.py:29
  13.6 1.1 %collective-permute-done.3.recv_ref = bf16[4,7,48,128]{3,2,1,0:T(8,128)(2,1)S(1)} collective-permute-done((bf16[4,7,48,128]{3,2,1,0:T(8,128)(2,1)S(1)}, bf16[4,7,48,128]{3,2,1,0:T(8,128)(2,1)S(1)}, u32[]{:S(2)}, u32[]{:S(2)}) %collective-permute-start.3) | collective-permute-done | bytes 344096 | tf_op jit(solution)/shard_map/ppermute | solution.py:16
  14.6 0.1 shard_map.73
  14.7 1.6 %collective-permute-start.4 = (bf16[7,48,128]{2,1,0:T(8,128)(2,1)S(1)}, bf16[7,48,128]{2,1,0:T(8,128)(2,1)S(1)}, u32[]{:S(2)}, u32[]{:S(2)}) collective-permute-start(bf16[7,48,128]{2,1,0:T(8,128)(2,1)S(1)} %get-tuple-element.24), channel_id=1, source_target_pairs={{0,2},{1,3},{2,0},{3,1},{4,6},{5,7},{6,4},{7,5},{8,10},{9,11},{10,... | collective-permute-start | bytes 258056 | tf_op jit(solution)/shard_map/ppermute | solution.py:16
  16.4 2.6 %collective-permute-start.5 = (bf16[7,48,128]{2,1,0:T(8,128)(2,1)S(1)}, bf16[7,48,128]{2,1,0:T(8,128)(2,1)S(1)}, u32[]{:S(2)}, u32[]{:S(2)}) collective-permute-start(bf16[7,48,128]{2,1,0:T(8,128)(2,1)S(1)} %get-tuple-element.25), channel_id=1, source_target_pairs={{0,4},{1,5},{2,6},{3,7},{4,0},{5,1},{6,2},{7,3},{8,12},{9,13},{10,... | collective-permute-start | bytes 258056 | tf_op jit(solution)/shard_map/ppermute | solution.py:16
  19.0 0.2 collective-permute-start.6
  19.2 0.2 collective-permute-done.4.refs_1_
  19.4 6.8 %collective-permute-done.5.refs_2_ = bf16[7,48,128]{2,1,0:T(8,128)(2,1)S(1)} collective-permute-done((bf16[7,48,128]{2,1,0:T(8,128)(2,1)S(1)}, bf16[7,48,128]{2,1,0:T(8,128)(2,1)S(1)}, u32[]{:S(2)}, u32[]{:S(2)}) %collective-permute-start.5) | collective-permute-done | bytes 86048 | tf_op jit(solution)/shard_map/ppermute | solution.py:16
  26.1 0.0 collective-permute-done.6.refs_3_
  26.1 0.1 shard_map.74.refs_0_
  26.2 2.2 %collective-permute-start.9 = (bf16[7,48,128]{2,1,0:T(8,128)(2,1)S(1)}, bf16[7,48,128]{2,1,0:T(8,128)(2,1)S(1)}, u32[]{:S(2)}, u32[]{:S(2)}) collective-permute-start(bf16[7,48,128]{2,1,0:T(8,128)(2,1)S(1)} %shard_map.74.refs_0_), channel_id=1, source_target_pairs={{0,24},{8,16},{16,8},{24,0},{1,25},{9,17},{17,9},{25,1},{2,26},{10... | collective-permute-start | bytes 258056 | tf_op jit(solution)/shard_map/ppermute | solution.py:16
  28.4 0.8 %collective-permute-start.8 = (bf16[7,48,128]{2,1,0:T(8,128)(2,1)S(1)}, bf16[7,48,128]{2,1,0:T(8,128)(2,1)S(1)}, u32[]{:S(2)}, u32[]{:S(2)}) collective-permute-start(bf16[7,48,128]{2,1,0:T(8,128)(2,1)S(1)} %shard_map.74.refs_0_), channel_id=1, source_target_pairs={{0,16},{8,24},{16,0},{24,8},{1,17},{9,25},{17,1},{25,9},{2,18},{10... | collective-permute-start | bytes 258056 | tf_op jit(solution)/shard_map/ppermute | solution.py:16
  29.2 0.6 %collective-permute-start.7 = (bf16[7,48,128]{2,1,0:T(8,128)(2,1)S(1)}, bf16[7,48,128]{2,1,0:T(8,128)(2,1)S(1)}, u32[]{:S(2)}, u32[]{:S(2)}) collective-permute-start(bf16[7,48,128]{2,1,0:T(8,128)(2,1)S(1)} %shard_map.74.refs_0_), channel_id=1, source_target_pairs={{0,8},{8,0},{16,24},{24,16},{1,9},{9,1},{17,25},{25,17},{2,10},{10... | collective-permute-start | bytes 258056 | tf_op jit(solution)/shard_map/ppermute | solution.py:16
  29.8 1.3 %shard_map.71 = bf16[64,256]{1,0:T(8,128)(2,1)} custom-call(bf16[9,18,16,128]{3,2,1,0:T(8,128)(2,1)S(1)} %get-tuple-element.18.refs_0_.refs_3_, bf16[27,256,128]{2,1,0:T(8,128)(2,1)S(1)} %get-tuple-element.16.refs_4_.refs_1_), custom_call_target="tpu_custom_call" | custom-call | tf_op jit(solution)/shard_map/pallas_call | solution.py:29
  31.0 0.6 %collective-permute-done.9.refs_3_ = bf16[7,48,128]{2,1,0:T(8,128)(2,1)S(1)} collective-permute-done((bf16[7,48,128]{2,1,0:T(8,128)(2,1)S(1)}, bf16[7,48,128]{2,1,0:T(8,128)(2,1)S(1)}, u32[]{:S(2)}, u32[]{:S(2)}) %collective-permute-start.9) | collective-permute-done | bytes 86048 | tf_op jit(solution)/shard_map/ppermute | solution.py:16
  31.7 1.2 %collective-permute-done.8.refs_2_ = bf16[7,48,128]{2,1,0:T(8,128)(2,1)S(1)} collective-permute-done((bf16[7,48,128]{2,1,0:T(8,128)(2,1)S(1)}, bf16[7,48,128]{2,1,0:T(8,128)(2,1)S(1)}, u32[]{:S(2)}, u32[]{:S(2)}) %collective-permute-start.8) | collective-permute-done | bytes 86048 | tf_op jit(solution)/shard_map/ppermute | solution.py:16
  32.9 0.8 %collective-permute-done.7.refs_1_ = bf16[7,48,128]{2,1,0:T(8,128)(2,1)S(1)} collective-permute-done((bf16[7,48,128]{2,1,0:T(8,128)(2,1)S(1)}, bf16[7,48,128]{2,1,0:T(8,128)(2,1)S(1)}, u32[]{:S(2)}, u32[]{:S(2)}) %collective-permute-start.7) | collective-permute-done | bytes 86048 | tf_op jit(solution)/shard_map/ppermute | solution.py:16
  33.7 1.0 %shard_map.75 = (f32[27,32,128]{2,1,0:T(8,128)}, f32[27,16,128]{2,1,0:T(8,128)}) custom-call(bf16[7,48,128]{2,1,0:T(8,128)(2,1)S(1)} %shard_map.74.refs_0_, bf16[7,48,128]{2,1,0:T(8,128)(2,1)S(1)} %collective-permute-done.7.refs_1_, bf16[7,48,128]{2,1,0:T(8,128)(2,1)S(1)} %collective-permute-done.8.refs_2_, ...), custom_call_target="tpu_custom_call" | custom-call | tf_op jit(solution)/shard_map/pallas_call | solution.py:29
Async XLA Ops:
  1.5 7.2 %collective-permute-start.2 = (bf16[4,96,128]{2,1,0:T(8,128)(2,1)S(1)}, bf16[4,96,128]{2,1,0:T(8,128)(2,1)S(1)}, u32[]{:S(2)}, u32[]{:S(2)}) collective-permute-start(bf16[4,96,128]{2,1,0:T(8,128)(2,1)S(1)} %shard_map.67.refs_0_), channel_id=1, source_target_pairs={{0,24},{8,16},{16,8},{24,0},{1,25},{9,17},{17,9},{25,1},{2,26},{10... | collective-permute-start | bytes 294920 | tf_op jit(solution)/shard_map/ppermute | solution.py:16
  5.5 4.9 %collective-permute-start.1 = (bf16[4,96,128]{2,1,0:T(8,128)(2,1)S(1)}, bf16[4,96,128]{2,1,0:T(8,128)(2,1)S(1)}, u32[]{:S(2)}, u32[]{:S(2)}) collective-permute-start(bf16[4,96,128]{2,1,0:T(8,128)(2,1)S(1)} %shard_map.67.refs_0_), channel_id=1, source_target_pairs={{0,16},{8,24},{16,0},{24,8},{1,17},{9,25},{17,1},{25,9},{2,18},{10... | collective-permute-start | bytes 294920 | tf_op jit(solution)/shard_map/ppermute | solution.py:16
  6.0 4.7 %collective-permute-start = (bf16[4,96,128]{2,1,0:T(8,128)(2,1)S(1)}, bf16[4,96,128]{2,1,0:T(8,128)(2,1)S(1)}, u32[]{:S(2)}, u32[]{:S(2)}) collective-permute-start(bf16[4,96,128]{2,1,0:T(8,128)(2,1)S(1)} %shard_map.67.refs_0_), channel_id=1, source_target_pairs={{0,8},{8,0},{16,24},{24,16},{1,9},{9,1},{17,25},{25,17},{2,10},{10... | collective-permute-start | bytes 294920 | tf_op jit(solution)/shard_map/ppermute | solution.py:16
  12.9 1.7 %collective-permute-start.3 = (bf16[4,7,48,128]{3,2,1,0:T(8,128)(2,1)S(1)}, bf16[4,7,48,128]{3,2,1,0:T(8,128)(2,1)S(1)}, u32[]{:S(2)}, u32[]{:S(2)}) collective-permute-start(bf16[4,7,48,128]{3,2,1,0:T(8,128)(2,1)S(1)} %get-tuple-element.22), channel_id=1, source_target_pairs={{0,1},{1,0},{2,3},{3,2},{4,5},{5,4},{6,7},{7,6},{8,9},{9,8},{10,11... | collective-permute-start | bytes 1032200 | tf_op jit(solution)/shard_map/ppermute | solution.py:16
  14.7 4.6 %collective-permute-start.4 = (bf16[7,48,128]{2,1,0:T(8,128)(2,1)S(1)}, bf16[7,48,128]{2,1,0:T(8,128)(2,1)S(1)}, u32[]{:S(2)}, u32[]{:S(2)}) collective-permute-start(bf16[7,48,128]{2,1,0:T(8,128)(2,1)S(1)} %get-tuple-element.24), channel_id=1, source_target_pairs={{0,2},{1,3},{2,0},{3,1},{4,6},{5,7},{6,4},{7,5},{8,10},{9,11},{10,... | collective-permute-start | bytes 258056 | tf_op jit(solution)/shard_map/ppermute | solution.py:16
  16.4 9.8 %collective-permute-start.5 = (bf16[7,48,128]{2,1,0:T(8,128)(2,1)S(1)}, bf16[7,48,128]{2,1,0:T(8,128)(2,1)S(1)}, u32[]{:S(2)}, u32[]{:S(2)}) collective-permute-start(bf16[7,48,128]{2,1,0:T(8,128)(2,1)S(1)} %get-tuple-element.25), channel_id=1, source_target_pairs={{0,4},{1,5},{2,6},{3,7},{4,0},{5,1},{6,2},{7,3},{8,12},{9,13},{10,... | collective-permute-start | bytes 258056 | tf_op jit(solution)/shard_map/ppermute | solution.py:16
  19.0 7.2 %collective-permute-start.6 = (bf16[7,48,128]{2,1,0:T(8,128)(2,1)S(1)}, bf16[7,48,128]{2,1,0:T(8,128)(2,1)S(1)}, u32[]{:S(2)}, u32[]{:S(2)}) collective-permute-start(bf16[7,48,128]{2,1,0:T(8,128)(2,1)S(1)} %get-tuple-element.26), channel_id=1, source_target_pairs={{0,6},{1,7},{2,4},{3,5},{4,2},{5,3},{6,0},{7,1},{8,14},{9,15},{10,... | collective-permute-start | bytes 258056 | tf_op jit(solution)/shard_map/ppermute | solution.py:16
  26.2 5.5 %collective-permute-start.9 = (bf16[7,48,128]{2,1,0:T(8,128)(2,1)S(1)}, bf16[7,48,128]{2,1,0:T(8,128)(2,1)S(1)}, u32[]{:S(2)}, u32[]{:S(2)}) collective-permute-start(bf16[7,48,128]{2,1,0:T(8,128)(2,1)S(1)} %shard_map.74.refs_0_), channel_id=1, source_target_pairs={{0,24},{8,16},{16,8},{24,0},{1,25},{9,17},{17,9},{25,1},{2,26},{10... | collective-permute-start | bytes 258056 | tf_op jit(solution)/shard_map/ppermute | solution.py:16
  28.4 4.5 %collective-permute-start.8 = (bf16[7,48,128]{2,1,0:T(8,128)(2,1)S(1)}, bf16[7,48,128]{2,1,0:T(8,128)(2,1)S(1)}, u32[]{:S(2)}, u32[]{:S(2)}) collective-permute-start(bf16[7,48,128]{2,1,0:T(8,128)(2,1)S(1)} %shard_map.74.refs_0_), channel_id=1, source_target_pairs={{0,16},{8,24},{16,0},{24,8},{1,17},{9,25},{17,1},{25,9},{2,18},{10... | collective-permute-start | bytes 258056 | tf_op jit(solution)/shard_map/ppermute | solution.py:16
  29.2 4.5 %collective-permute-start.7 = (bf16[7,48,128]{2,1,0:T(8,128)(2,1)S(1)}, bf16[7,48,128]{2,1,0:T(8,128)(2,1)S(1)}, u32[]{:S(2)}, u32[]{:S(2)}) collective-permute-start(bf16[7,48,128]{2,1,0:T(8,128)(2,1)S(1)} %shard_map.74.refs_0_), channel_id=1, source_target_pairs={{0,8},{8,0},{16,24},{24,16},{1,9},{9,1},{17,25},{25,17},{2,10},{10... | collective-permute-start | bytes 258056 | tf_op jit(solution)/shard_map/ppermute | solution.py:16

commit v5 on v4

--- a/solution.py
+++ b/solution.py
@@ -16,12 +16,13 @@
     return lax.ppermute(value, axis, [(i, i ^ (hop * stride)) for i in range(size)])
 
 
-def call(body, out_shape, scratch=(), grant=8, far=0):
+def call(body, out_shape, scratch=(), grant=8, far=0, alias=None):
     options = {"in_specs": [pl.BlockSpec(memory_space=pltpu.HBM)] * far} if far else {}
     kernel = pl.pallas_call(
         body,
         out_shape=out_shape,
         scratch_shapes=list(scratch),
+        input_output_aliases=alias or {},
         compiler_params=pltpu.CompilerParams(vmem_limit_bytes=grant << 20),
         **options,
     )
@@ -102,14 +103,32 @@
     return lax.dot_general(ups, weight, (((1,), (1,)), ((), ())), preferred_element_type=F32)
 
 
-def early_kernel(dims, one, two, w2_ref, out_ref, uc):
-    hi, wi, skip = dims
-    frames = one.shape[0]
+def place(dims, hop, block, xs, uc):
+    _, hi, wi, parts = dims
+    frames, _, _ = block.shape
+    low = hi * wi
+    start = (lax.axis_index("tm") ^ hop) * frames
+    feats = jnp.concatenate([rows_of(block[:, part * low : (part + 1) * low, :]) for part in range(parts)], axis=1)
+    xs[pl.ds(pl.multiple_of((start + 2) * low, low), frames * low), :] = feats
+    for e, value in enumerate(shifted(block, parts * low, 2 * hi, wi)):
+        uc[e, pl.ds(start, frames), 1 : 2 * hi + 1] = value
+    return start
+
+
+def add_second(starts, frames, w2_ref, uc, zs):
+    found = through_second(uc, starts, frames, w2_ref).reshape((len(starts), frames) + zs.shape[1:])
+    for at, start in enumerate(starts):
+        zs[pl.ds(start, frames)] = found[at]
+
+
+def early_kernel(dims, one, two, w2_ref, zs, uc, xs):
+    tm, hi, wi, _ = dims
+    total, low = zs.shape[0], hi * wi
+    xs[: 2 * low] = jnp.zeros((2 * low, xs.shape[1]), BF16)
+    uc[:, total:] = jnp.zeros((3, 2) + uc.shape[2:], BF16)
     clear_edges(uc)
-    for at, block in enumerate((one, two)):
-        for e, value in enumerate(shifted(block, skip, 2 * hi, wi)):
-            uc[e, at * frames : (at + 1) * frames, 1 : 2 * hi + 1] = value
-    out_ref[...] = through_second(uc, [0], 2 * frames, w2_ref)
+    starts = [place(dims, hop, block, xs, uc) for hop, block in ((0, one), (tm - 1, two))]
+    add_second(starts, one.shape[0], w2_ref, uc, zs)
 
 
 def kernel_grads(dims, same_core, ft, ht, uc, dbox_ref, out_ref):
@@ -149,79 +168,61 @@
                 out_ref[hop, j + k, :tall] = part.astype(out_ref.dtype)
 
 
-def main_kernel(dims, blocks, w1_ref, w2_ref, early_ref, send_ref, ft, ht, uc, dbox_ref, xs, zs):
+def main_kernel(dims, blocks, w1_ref, w2_ref, send_ref, ft, ht, dbox_ref, zs, uc, xs, sums, slopes):
     tm, _, hi, wi, _ = dims
     ho, wo = 2 * hi, 2 * wi
     low = hi * wi
-    frames = blocks[0].shape[0]
-    total = frames * tm
+    total = zs.shape[0]
     cin, cout = w1_ref.shape[1], w1_ref.shape[2]
-    parts = cin // cout
-    me = lax.axis_index("tm")
-
-    xs[: 2 * low] = jnp.zeros((2 * low, cin), BF16)
-    uc[:, total:] = jnp.zeros((3, 2) + uc.shape[2:], BF16)
-    clear_edges(uc)
-    starts = [(me ^ hop) * frames for hop in range(tm)]
-    for start, block in zip(starts, blocks):
-        feats = jnp.concatenate(
-            [rows_of(block[:, part * low : (part + 1) * low, :]) for part in range(parts)], axis=1
-        )
-        xs[pl.ds(pl.multiple_of((start + 2) * low, low), frames * low), :] = feats
-        for e, value in enumerate(shifted(block, parts * low, ho, wi)):
-            uc[e, pl.ds(start, frames), 1 : ho + 1] = value
+    starts = [place((tm, hi, wi, cin // cout), hop, block, xs, uc) for hop, block in enumerate(blocks, 1)]
 
     stacked = jnp.concatenate([xs[a * low : (a + total) * low, :] for a in range(3)], axis=1)
     weight = jnp.concatenate(
         [jnp.concatenate([w1_ref[a * 9 + be] for be in range(9)], axis=1) for a in range(3)], axis=0
     )
-    sums = jnp.dot(stacked, weight, preferred_element_type=F32).reshape(total, hi, wi, 9 * cout)
-    by_row = [sums[..., b * 3 * cout : (b + 1) * 3 * cout] for b in range(3)]
-    zero = jnp.zeros((total, wi, 3 * cout), F32)
-    pre_rows = []
-    for row in range(hi):
-        up = by_row[0][:, row - 1] if row else zero
-        down = by_row[2][:, row + 1] if row + 1 < hi else zero
-        pre_rows.append(up + by_row[1][:, row] + by_row[2][:, row])
-        pre_rows.append(by_row[0][:, row] + by_row[1][:, row] + down)
-    sums = jnp.stack(pre_rows, axis=1)
-    first, middle, last = (sums[..., e * cout : (e + 1) * cout] for e in range(3))
-    even = move_down(first, 0) + middle + last
-    odd = first + middle + move_down(last, wi - 1)
-    pre = jnp.concatenate([even, odd], axis=2)
-    sigma = 1.0 / (1.0 + jnp.exp(-pre))
-    hidden = pre * sigma
-    slope = sigma * (1.0 + pre * (1.0 - sigma))
-    ht[...] = rows_of(hidden).T.reshape(ht.shape)
+    sums[...] = jnp.dot(stacked, weight, preferred_element_type=F32).reshape(sums.shape)
+    zero = jnp.zeros((wi, 3 * cout), F32)
+    group = 128 // (ho * wo)
+    for t in range(0, total, group):
+        hidden = []
+        for at in range(t, t + group):
+            by_row = [
+                [sums[at, row, :, b * 3 * cout : (b + 1) * 3 * cout] for row in range(hi)] for b in range(3)
+            ]
+            pre_rows = []
+            for row in range(hi):
+                up = by_row[0][row - 1] if row else zero
+                down = by_row[2][row + 1] if row + 1 < hi else zero
+                pre_rows.append(up + by_row[1][row] + by_row[2][row])
+                pre_rows.append(by_row[0][row] + by_row[1][row] + down)
+            rows = jnp.stack(pre_rows, axis=0)
+            first, middle, last = (rows[..., e * cout : (e + 1) * cout] for e in range(3))
+            even = move_down(first, 0) + middle + last
+            odd = first + middle + move_down(last, wi - 1)
+            pre = jnp.concatenate([even, odd], axis=1)
+            sigma = 1.0 / (1.0 + jnp.exp(-pre))
+            hidden.append(rows_of(pre * sigma))
+            slopes[at] = sigma * (1.0 + pre * (1.0 - sigma))
+        turned = jnp.concatenate(hidden, axis=0).T
+        ht[:, :, t * ho * wo : (t + group) * ho * wo] = turned.reshape(ht.shape[:2] + turned.shape[1:])
     ft[...] = xs[2 * low :, :].astype(F32).T.reshape(ft.shape)
 
-    late = starts[1:-1]
-    for found, places in ((through_second(uc, late, frames, w2_ref), late), (early_ref[...], starts[:: tm - 1])):
-        found = found.reshape(len(places), frames, ho, wo, 3 * cout)
-        for at, start in enumerate(places):
-            zs[pl.ds(start, frames)] = found[at]
-    parts_of = zs[...]
-    back = parts_of[..., 2 * cout :]
-    for a in range(2):
-        lead = 2 - a
-        term = parts_of[lead:, ..., a * cout : (a + 1) * cout]
-        back += jnp.concatenate([term, jnp.zeros((lead,) + term.shape[1:], F32)], axis=0)
-    dpre = (back.reshape(slope.shape) * slope).astype(BF16).astype(F32)
-    even, odd = dpre[:, :, :wi], dpre[:, :, wi:]
-    columns = (odd + move_down(even, wi - 1), even + odd, move_down(odd, 0) + even)
-    for e in range(3):
-        col = columns[e]
-        for b in range(3):
-            picked = []
-            for row in range(hi):
-                one, two = 2 * row + 1 - b, 2 * row + 2 - b
-                value = None
-                for at in (one, two):
-                    if 0 <= at < ho:
-                        value = col[:, at] if value is None else value + col[:, at]
-                picked.append(value)
-            box = jnp.concatenate(picked, axis=1)
-            dbox_ref[b * 3 + e, :total] = box.astype(BF16)
+    add_second(starts, blocks[0].shape[0], w2_ref, uc, zs)
+    for t in range(total):
+        back = zs[t, :, :, 2 * cout :]
+        for a in range(2):
+            if t + 2 - a < total:
+                back += zs[t + 2 - a, :, :, a * cout : (a + 1) * cout]
+        dpre = (back * slopes[t]).astype(BF16).astype(F32)
+        even, odd = dpre[:, :wi], dpre[:, wi:]
+        columns = (odd + move_down(even, wi - 1), even + odd, move_down(odd, 0) + even)
+        for e, col in enumerate(columns):
+            for b in range(3):
+                picked = []
+                for row in range(hi):
+                    near = [col[at] for at in (2 * row + 1 - b, 2 * row + 2 - b) if 0 <= at < ho]
+                    picked.append(sum(near[1:], near[0]))
+                dbox_ref[b * 3 + e, t] = jnp.concatenate(picked, axis=0).astype(BF16)
     dbox_ref[:, total:] = jnp.zeros((9, 2, low, cout), BF16)
 
     kernel_grads(dims, False, ft, ht, uc, dbox_ref, send_ref)
@@ -304,36 +305,40 @@
         far=2,
     )(w1, w2)
 
+    shared = (
+        near((total, ho, wo, 3 * cout), F32),
+        near((3, total + 2, ho + 2, wo, cout), BF16),
+        near(((total + 2) * low, cin), BF16),
+    )
     early = call(
-        lambda *refs: early_kernel((hi, wi, low * (cin // cout)), *refs),
-        near((2 * frames * high, 3 * cout), F32),
-        [pltpu.VMEM((3, 2 * frames, ho + 2, wo, cout), BF16)],
+        lambda *refs: early_kernel((tm, hi, wi, cin // cout), *refs), shared, grant=12
     )(blocks[0], blocks[-1], w2)
 
     def main_body(*refs):
-        main_kernel((tm, dp, hi, wi, chunk), refs[:tm], *refs[tm:])
-
-    send, *held = call(
+        late = tm - 2
+        main_kernel((tm, dp, hi, wi, chunk), refs[:late], *refs[late : late + 2], *refs[late + 5 :])
+
+    send, ft, ht, dbox, _, held, _ = call(
         main_body,
         (
             near((far_size, chunk, tall + short, cout), BF16),
             near((dp, tall, total * low), F32),
             near((dp, short, total * high), F32),
-            near((3, total + 2, ho + 2, wo, cout), BF16),
             near((9, total + 2, low, cout), BF16),
-        ),
+        )
+        + shared,
         [
-            pltpu.VMEM(((total + 2) * low, cin), BF16),
-            pltpu.VMEM((total, ho, wo, 3 * cout), F32),
+            pltpu.VMEM((total, hi, wi, 9 * cout), F32),
+            pltpu.VMEM((total, ho, wo, cout), F32),
         ],
         grant=32,
-    )(*blocks, w1, w2, early)
-    dbox = held[-1]
+        alias={tm: 4, tm + 1: 5, tm + 2: 6},
+    )(*blocks[1:-1], w1, w2, *early)
 
     keep = call(
         lambda *refs: kernel_grads((tm, dp, hi, wi, chunk), True, *refs),
         near((far_size, chunk, tall + short, cout), F32),
-    )(*held)
+    )(ft, ht, held, dbox)
     recv = swap(send, "dp", 1)
     own, *sends = call(
         pair_kernel,

time: 34.8 us -> 34.7 us (level)
  no operation moved by 1% of the time
where the time goes in v5:
time: 34.7 us; the launch traced here: 34.5 us
  starting transfers between devices  12.7 us (37%)
  waiting for transfers between devices  12.6 us (36%)
  Pallas kernels  8.49 us (24%)
  between operations  0.69 us (2%)
    ppermute x10, starting transfers between devices, swap(): lax.ppermute(value, axis, [(i, i ^ hop * stride) for i in range(size)])  12.7 us
    ppermute x10, waiting for transfers between devices, swap(): lax.ppermute(value, axis, [(i, i ^ hop * stride) for i in range(size)])  12.6 us
    pallas_call x9, Pallas kernels, call(): kernel(*(pltpu.with_memory_space_constraint(v, space) for v in values))  8.49 us
  transfers between devices with their start and end apart: 10, of which 9 were waited for; matrix products, arithmetic and copies ran while one was open for 0% of the time, Pallas kernels for 13%

profile of v5, /device:TPU:0, one launch (start us, length us, event | category | flops | bytes accessed | tf_op | source)
XLA Modules:
  0.0 34.5 jit_solution(3521170450235198762)
XLA Ops:
  0.6 0.9 %shard_map.67.refs_0_ = bf16[4,96,128]{2,1,0:T(8,128)(2,1)S(1)} custom-call(bf16[4,16,256]{2,1,0:T(8,128)(2,1)} %bitcast.11, bf16[4,4,16,128]{3,2,1,0:T(8,128)(2,1)} %bitcast.9), custom_call_target="tpu_custom_call" | custom-call | tf_op jit(solution)/shard_map/pallas_call | solution.py:30
  1.5 4.0 %collective-permute-start.2 = (bf16[4,96,128]{2,1,0:T(8,128)(2,1)S(1)}, bf16[4,96,128]{2,1,0:T(8,128)(2,1)S(1)}, u32[]{:S(2)}, u32[]{:S(2)}) collective-permute-start(bf16[4,96,128]{2,1,0:T(8,128)(2,1)S(1)} %shard_map.67.refs_0_), channel_id=1, source_target_pairs={{0,24},{8,16},{16,8},{24,0},{1,25},{9,17},{17,9},{25,1},{2,26},{10... | collective-permute-start | bytes 294920 | tf_op jit(solution)/shard_map/ppermute | solution.py:16
  5.5 0.5 %collective-permute-start.1 = (bf16[4,96,128]{2,1,0:T(8,128)(2,1)S(1)}, bf16[4,96,128]{2,1,0:T(8,128)(2,1)S(1)}, u32[]{:S(2)}, u32[]{:S(2)}) collective-permute-start(bf16[4,96,128]{2,1,0:T(8,128)(2,1)S(1)} %shard_map.67.refs_0_), channel_id=1, source_target_pairs={{0,16},{8,24},{16,0},{24,8},{1,17},{9,25},{17,1},{25,9},{2,18},{10... | collective-permute-start | bytes 294920 | tf_op jit(solution)/shard_map/ppermute | solution.py:16
  6.0 0.1 collective-permute-start
  6.2 1.7 %shard_map.68 = (bf16[27,256,128]{2,1,0:T(8,128)(2,1)S(1)}, bf16[27,128,128]{2,1,0:T(8,128)(2,1)S(1)}) custom-call(bf16[27,256,128]{2,1,0:T(8,128)(2,1)} %bitcast.7, bf16[27,128,128]{2,1,0:T(8,128)(2,1)} %bitcast.8), custom_call_target="tpu_custom_call" | custom-call | tf_op jit(solution)/shard_map/pallas_call | solution.py:30
  7.9 0.8 %collective-permute-done.2.refs_1_ = bf16[4,96,128]{2,1,0:T(8,128)(2,1)S(1)} collective-permute-done((bf16[4,96,128]{2,1,0:T(8,128)(2,1)S(1)}, bf16[4,96,128]{2,1,0:T(8,128)(2,1)S(1)}, u32[]{:S(2)}, u32[]{:S(2)}) %collective-permute-start.2) | collective-permute-done | bytes 98336 | tf_op jit(solution)/shard_map/ppermute | solution.py:16
  8.7 0.9 %shard_map.69 = (f32[16,4,16,384]{3,2,1,0:T(8,128)S(1)}, bf16[3,18,6,16,128]{4,3,2,1,0:T(8,128)(2,1)S(1)}, bf16[288,256]{1,0:T(8,128)(2,1)S(1)}) custom-call(bf16[4,96,128]{2,1,0:T(8,128)(2,1)S(1)} %shard_map.67.refs_0_, bf16[4,96,128]{2,1,0:T(8,128)(2,1)S(1)} %collective-permute-done.2.refs_1_, bf16[27,128,128]{2,1,0:T(8,128)(2,1)S(1)} %get-tuple-element.20.refs_2_.refs_3_), custom_call_target="tpu_custom_call" | custom-call | tf_op jit(solution)/shard_map/pallas_call | solution.py:30
  9.6 0.8 %collective-permute-done.1.refs_1_ = bf16[4,96,128]{2,1,0:T(8,128)(2,1)S(1)} collective-permute-done((bf16[4,96,128]{2,1,0:T(8,128)(2,1)S(1)}, bf16[4,96,128]{2,1,0:T(8,128)(2,1)S(1)}, u32[]{:S(2)}, u32[]{:S(2)}) %collective-permute-start.1) | collective-permute-done | bytes 98336 | tf_op jit(solution)/shard_map/ppermute | solution.py:16
  10.4 0.3 collective-permute-done.refs_0_
  10.8 2.1 %shard_map.70 = (bf16[4,7,48,128]{3,2,1,0:T(8,128)(2,1)S(1)}, f32[8,32,256]{2,1,0:T(8,128)S(1)}, f32[8,16,1024]{2,1,0:T(8,128)S(1)}, bf16[9,18,16,128]{3,2,1,0:T...) custom-call(bf16[4,96,128]{2,1,0:T(8,128)(2,1)S(1)} %collective-perm, ...), custom_call_target="tpu_custom_call", output_to_operand_aliasing={{4}: (4, {}), {5}: (5, {}), {6}: (6, {})} | custom-call | tf_op jit(solution)/shard_map/pallas_call | solution.py:30
  12.8 0.1 collective-permute-start.3
  12.9 0.6 %shard_map.72.keep_ref = f32[4,7,48,128]{3,2,1,0:T(8,128)S(1)} custom-call(f32[8,32,256]{2,1,0:T(8,128)S(1)} %get-tuple-element.25.refs_0_, f32[8,16,1024]{2,1,0:T(8,128)S(1)} %get-tuple-element.26.refs_1_, bf16[3,18,6,16,128]{4,3,2,1,0:T(8,128)(2,1)S(1)} %get-tuple-element.27.refs_2_, bf16[9,18,16,128]{3,2,1,0:T(8,128)(2,1)S(1)} %get-tuple-element.24.refs_0_.refs_3_), custom_call_target="tpu_custom_call" | custom-call | tf_op jit(solution)/shard_map/pallas_call | solution.py:30
  13.5 1.1 %collective-permute-done.3.recv_ref = bf16[4,7,48,128]{3,2,1,0:T(8,128)(2,1)S(1)} collective-permute-done((bf16[4,7,48,128]{3,2,1,0:T(8,128)(2,1)S(1)}, bf16[4,7,48,128]{3,2,1,0:T(8,128)(2,1)S(1)}, u32[]{:S(2)}, u32[]{:S(2)}) %collective-permute-start.3) | collective-permute-done | bytes 344096 | tf_op jit(solution)/shard_map/ppermute | solution.py:16
  14.5 0.1 shard_map.73
  14.6 1.6 %collective-permute-start.4 = (bf16[7,48,128]{2,1,0:T(8,128)(2,1)S(1)}, bf16[7,48,128]{2,1,0:T(8,128)(2,1)S(1)}, u32[]{:S(2)}, u32[]{:S(2)}) collective-permute-start(bf16[7,48,128]{2,1,0:T(8,128)(2,1)S(1)} %get-tuple-element.30), channel_id=1, source_target_pairs={{0,2},{1,3},{2,0},{3,1},{4,6},{5,7},{6,4},{7,5},{8,10},{9,11},{10,... | collective-permute-start | bytes 258056 | tf_op jit(solution)/shard_map/ppermute | solution.py:16
  16.2 2.6 %collective-permute-start.5 = (bf16[7,48,128]{2,1,0:T(8,128)(2,1)S(1)}, bf16[7,48,128]{2,1,0:T(8,128)(2,1)S(1)}, u32[]{:S(2)}, u32[]{:S(2)}) collective-permute-start(bf16[7,48,128]{2,1,0:T(8,128)(2,1)S(1)} %get-tuple-element.31), channel_id=1, source_target_pairs={{0,4},{1,5},{2,6},{3,7},{4,0},{5,1},{6,2},{7,3},{8,12},{9,13},{10,... | collective-permute-start | bytes 258056 | tf_op jit(solution)/shard_map/ppermute | solution.py:16
  18.8 0.2 collective-permute-start.6
  19.1 0.2 collective-permute-done.4.refs_1_
  19.2 6.8 %collective-permute-done.5.refs_2_ = bf16[7,48,128]{2,1,0:T(8,128)(2,1)S(1)} collective-permute-done((bf16[7,48,128]{2,1,0:T(8,128)(2,1)S(1)}, bf16[7,48,128]{2,1,0:T(8,128)(2,1)S(1)}, u32[]{:S(2)}, u32[]{:S(2)}) %collective-permute-start.5) | collective-permute-done | bytes 86048 | tf_op jit(solution)/shard_map/ppermute | solution.py:16
  26.0 0.0 collective-permute-done.6.refs_3_
  26.0 0.1 shard_map.74.refs_0_
  26.1 2.3 %collective-permute-start.9 = (bf16[7,48,128]{2,1,0:T(8,128)(2,1)S(1)}, bf16[7,48,128]{2,1,0:T(8,128)(2,1)S(1)}, u32[]{:S(2)}, u32[]{:S(2)}) collective-permute-start(bf16[7,48,128]{2,1,0:T(8,128)(2,1)S(1)} %shard_map.74.refs_0_), channel_id=1, source_target_pairs={{0,24},{8,16},{16,8},{24,0},{1,25},{9,17},{17,9},{25,1},{2,26},{10... | collective-permute-start | bytes 258056 | tf_op jit(solution)/shard_map/ppermute | solution.py:16
  28.3 0.7 %collective-permute-start.8 = (bf16[7,48,128]{2,1,0:T(8,128)(2,1)S(1)}, bf16[7,48,128]{2,1,0:T(8,128)(2,1)S(1)}, u32[]{:S(2)}, u32[]{:S(2)}) collective-permute-start(bf16[7,48,128]{2,1,0:T(8,128)(2,1)S(1)} %shard_map.74.refs_0_), channel_id=1, source_target_pairs={{0,16},{8,24},{16,0},{24,8},{1,17},{9,25},{17,1},{25,9},{2,18},{10... | collective-permute-start | bytes 258056 | tf_op jit(solution)/shard_map/ppermute | solution.py:16
  29.0 0.6 %collective-permute-start.7 = (bf16[7,48,128]{2,1,0:T(8,128)(2,1)S(1)}, bf16[7,48,128]{2,1,0:T(8,128)(2,1)S(1)}, u32[]{:S(2)}, u32[]{:S(2)}) collective-permute-start(bf16[7,48,128]{2,1,0:T(8,128)(2,1)S(1)} %shard_map.74.refs_0_), channel_id=1, source_target_pairs={{0,8},{8,0},{16,24},{24,16},{1,9},{9,1},{17,25},{25,17},{2,10},{10... | collective-permute-start | bytes 258056 | tf_op jit(solution)/shard_map/ppermute | solution.py:16
  29.6 1.3 %shard_map.71 = bf16[64,256]{1,0:T(8,128)(2,1)} custom-call(bf16[9,18,16,128]{3,2,1,0:T(8,128)(2,1)S(1)} %get-tuple-element.24.refs_0_.refs_3_, bf16[27,256,128]{2,1,0:T(8,128)(2,1)S(1)} %get-tuple-element.19.refs_2_.refs_1_), custom_call_target="tpu_custom_call" | custom-call | tf_op jit(solution)/shard_map/pallas_call | solution.py:30
  30.9 0.7 %collective-permute-done.9.refs_3_ = bf16[7,48,128]{2,1,0:T(8,128)(2,1)S(1)} collective-permute-done((bf16[7,48,128]{2,1,0:T(8,128)(2,1)S(1)}, bf16[7,48,128]{2,1,0:T(8,128)(2,1)S(1)}, u32[]{:S(2)}, u32[]{:S(2)}) %collective-permute-start.9) | collective-permute-done | bytes 86048 | tf_op jit(solution)/shard_map/ppermute | solution.py:16
  31.6 1.2 %collective-permute-done.8.refs_2_ = bf16[7,48,128]{2,1,0:T(8,128)(2,1)S(1)} collective-permute-done((bf16[7,48,128]{2,1,0:T(8,128)(2,1)S(1)}, bf16[7,48,128]{2,1,0:T(8,128)(2,1)S(1)}, u32[]{:S(2)}, u32[]{:S(2)}) %collective-permute-start.8) | collective-permute-done | bytes 86048 | tf_op jit(solution)/shard_map/ppermute | solution.py:16
  32.8 0.7 %collective-permute-done.7.refs_1_ = bf16[7,48,128]{2,1,0:T(8,128)(2,1)S(1)} collective-permute-done((bf16[7,48,128]{2,1,0:T(8,128)(2,1)S(1)}, bf16[7,48,128]{2,1,0:T(8,128)(2,1)S(1)}, u32[]{:S(2)}, u32[]{:S(2)}) %collective-permute-start.7) | collective-permute-done | bytes 86048 | tf_op jit(solution)/shard_map/ppermute | solution.py:16
  33.5 1.0 %shard_map.75 = (f32[27,32,128]{2,1,0:T(8,128)}, f32[27,16,128]{2,1,0:T(8,128)}) custom-call(bf16[7,48,128]{2,1,0:T(8,128)(2,1)S(1)} %shard_map.74.refs_0_, bf16[7,48,128]{2,1,0:T(8,128)(2,1)S(1)} %collective-permute-done.7.refs_1_, bf16[7,48,128]{2,1,0:T(8,128)(2,1)S(1)} %collective-permute-done.8.refs_2_, ...), custom_call_target="tpu_custom_call" | custom-call | tf_op jit(solution)/shard_map/pallas_call | solution.py:30
Async XLA Ops:
  1.5 7.2 %collective-permute-start.2 = (bf16[4,96,128]{2,1,0:T(8,128)(2,1)S(1)}, bf16[4,96,128]{2,1,0:T(8,128)(2,1)S(1)}, u32[]{:S(2)}, u32[]{:S(2)}) collective-permute-start(bf16[4,96,128]{2,1,0:T(8,128)(2,1)S(1)} %shard_map.67.refs_0_), channel_id=1, source_target_pairs={{0,24},{8,16},{16,8},{24,0},{1,25},{9,17},{17,9},{25,1},{2,26},{10... | collective-permute-start | bytes 294920 | tf_op jit(solution)/shard_map/ppermute | solution.py:16
  5.5 4.9 %collective-permute-start.1 = (bf16[4,96,128]{2,1,0:T(8,128)(2,1)S(1)}, bf16[4,96,128]{2,1,0:T(8,128)(2,1)S(1)}, u32[]{:S(2)}, u32[]{:S(2)}) collective-permute-start(bf16[4,96,128]{2,1,0:T(8,128)(2,1)S(1)} %shard_map.67.refs_0_), channel_id=1, source_target_pairs={{0,16},{8,24},{16,0},{24,8},{1,17},{9,25},{17,1},{25,9},{2,18},{10... | collective-permute-start | bytes 294920 | tf_op jit(solution)/shard_map/ppermute | solution.py:16
  6.0 4.7 %collective-permute-start = (bf16[4,96,128]{2,1,0:T(8,128)(2,1)S(1)}, bf16[4,96,128]{2,1,0:T(8,128)(2,1)S(1)}, u32[]{:S(2)}, u32[]{:S(2)}) collective-permute-start(bf16[4,96,128]{2,1,0:T(8,128)(2,1)S(1)} %shard_map.67.refs_0_), channel_id=1, source_target_pairs={{0,8},{8,0},{16,24},{24,16},{1,9},{9,1},{17,25},{25,17},{2,10},{10... | collective-permute-start | bytes 294920 | tf_op jit(solution)/shard_map/ppermute | solution.py:16
  12.8 1.7 %collective-permute-start.3 = (bf16[4,7,48,128]{3,2,1,0:T(8,128)(2,1)S(1)}, bf16[4,7,48,128]{3,2,1,0:T(8,128)(2,1)S(1)}, u32[]{:S(2)}, u32[]{:S(2)}) collective-permute-start(bf16[4,7,48,128]{3,2,1,0:T(8,128)(2,1)S(1)} %get-tuple-element.28), channel_id=1, source_target_pairs={{0,1},{1,0},{2,3},{3,2},{4,5},{5,4},{6,7},{7,6},{8,9},{9,8},{10,11... | collective-permute-start | bytes 1032200 | tf_op jit(solution)/shard_map/ppermute | solution.py:16
  14.6 4.6 %collective-permute-start.4 = (bf16[7,48,128]{2,1,0:T(8,128)(2,1)S(1)}, bf16[7,48,128]{2,1,0:T(8,128)(2,1)S(1)}, u32[]{:S(2)}, u32[]{:S(2)}) collective-permute-start(bf16[7,48,128]{2,1,0:T(8,128)(2,1)S(1)} %get-tuple-element.30), channel_id=1, source_target_pairs={{0,2},{1,3},{2,0},{3,1},{4,6},{5,7},{6,4},{7,5},{8,10},{9,11},{10,... | collective-permute-start | bytes 258056 | tf_op jit(solution)/shard_map/ppermute | solution.py:16
  16.2 9.8 %collective-permute-start.5 = (bf16[7,48,128]{2,1,0:T(8,128)(2,1)S(1)}, bf16[7,48,128]{2,1,0:T(8,128)(2,1)S(1)}, u32[]{:S(2)}, u32[]{:S(2)}) collective-permute-start(bf16[7,48,128]{2,1,0:T(8,128)(2,1)S(1)} %get-tuple-element.31), channel_id=1, source_target_pairs={{0,4},{1,5},{2,6},{3,7},{4,0},{5,1},{6,2},{7,3},{8,12},{9,13},{10,... | collective-permute-start | bytes 258056 | tf_op jit(solution)/shard_map/ppermute | solution.py:16
  18.8 7.2 %collective-permute-start.6 = (bf16[7,48,128]{2,1,0:T(8,128)(2,1)S(1)}, bf16[7,48,128]{2,1,0:T(8,128)(2,1)S(1)}, u32[]{:S(2)}, u32[]{:S(2)}) collective-permute-start(bf16[7,48,128]{2,1,0:T(8,128)(2,1)S(1)} %get-tuple-element.32), channel_id=1, source_target_pairs={{0,6},{1,7},{2,4},{3,5},{4,2},{5,3},{6,0},{7,1},{8,14},{9,15},{10,... | collective-permute-start | bytes 258056 | tf_op jit(solution)/shard_map/ppermute | solution.py:16
  26.1 5.6 %collective-permute-start.9 = (bf16[7,48,128]{2,1,0:T(8,128)(2,1)S(1)}, bf16[7,48,128]{2,1,0:T(8,128)(2,1)S(1)}, u32[]{:S(2)}, u32[]{:S(2)}) collective-permute-start(bf16[7,48,128]{2,1,0:T(8,128)(2,1)S(1)} %shard_map.74.refs_0_), channel_id=1, source_target_pairs={{0,24},{8,16},{16,8},{24,0},{1,25},{9,17},{17,9},{25,1},{2,26},{10... | collective-permute-start | bytes 258056 | tf_op jit(solution)/shard_map/ppermute | solution.py:16
  28.3 4.5 %collective-permute-start.8 = (bf16[7,48,128]{2,1,0:T(8,128)(2,1)S(1)}, bf16[7,48,128]{2,1,0:T(8,128)(2,1)S(1)}, u32[]{:S(2)}, u32[]{:S(2)}) collective-permute-start(bf16[7,48,128]{2,1,0:T(8,128)(2,1)S(1)} %shard_map.74.refs_0_), channel_id=1, source_target_pairs={{0,16},{8,24},{16,0},{24,8},{1,17},{9,25},{17,1},{25,9},{2,18},{10... | collective-permute-start | bytes 258056 | tf_op jit(solution)/shard_map/ppermute | solution.py:16
  29.0 4.5 %collective-permute-start.7 = (bf16[7,48,128]{2,1,0:T(8,128)(2,1)S(1)}, bf16[7,48,128]{2,1,0:T(8,128)(2,1)S(1)}, u32[]{:S(2)}, u32[]{:S(2)}) collective-permute-start(bf16[7,48,128]{2,1,0:T(8,128)(2,1)S(1)} %shard_map.74.refs_0_), channel_id=1, source_target_pairs={{0,8},{8,0},{16,24},{24,16},{1,9},{9,1},{17,25},{25,17},{2,10},{10... | collective-permute-start | bytes 258056 | tf_op jit(solution)/shard_map/ppermute | solution.py:16
